TPU v7x, 32 devices: a whole 2x2x4 slice. The times are simulated.
32 devices in a mesh: groups: 2 (over x), chan: 16 (over z, y, core).
Axes of the slice: x: 2, y: 2, z: 4, core: 2. Of those that a mesh axis runs over, the one named last changes fastest.
Arguments:
- waveforms: bfloat16 [10240, 15360], P('chan', 'groups'), parts along dimension 1, may hold values from -250 to 250
- basis: bfloat16 [16, 10240, 200], P(None, 'chan'), may hold values from -1 to 1
- bounds: int32 [2, 768], replicated, may hold values from 0 to 5120, as said below
Outputs:
- detection: float32 [15360], P(('groups', 'chan')), parts along dimension 0
- coefficients: float32 [16, 15360], P(None, ('groups', 'chan')), parts along dimension 1
There are 2 independent parts, one for each index of `groups`. A program takes and returns all parts, laid end to end along the dimension named above; an argument that names none is the same for every part. Nothing has to cross between parts.
Inputs may be any that keep to these rules, and one draw needn't show every extreme that they name: bounds[0, 0] is 0 and every bounds[0, f] is below 160; bounds[1, f] grows roughly in proportion to f and is 5120 at the last bin; where bounds[0, f] exceeds bounds[1, f] nothing passes.
All inputs are finite; a program needn't handle non-finite values.
Results may differ from a plain program's by a relative error of at most 0.017.
Values may be sent and summed in bfloat16 or wider, within the bound.
A program may use at most 128 MiB of HBM per device.

v0:
```python
import math

import jax
import jax.numpy as jnp
from jax import lax
from jax.sharding import PartitionSpec as P

time_blocks = 4
basis_blocks = 4
highest = lax.Precision.HIGHEST


def angle_lookup(row_ids, col_ids, modulus):
    rotation_radians = (row_ids[:, None] * col_ids[None, :] % modulus).astype(jnp.float32) * (
        2.0 * math.pi / modulus
    )
    return (jnp.cos(rotation_radians), jnp.sin(rotation_radians))


def rotate(layout, cos_table, sin_table, real_part, imag_part, orientation):
    cos_real = jnp.einsum(layout, cos_table, real_part, precision=highest)
    cos_imag = jnp.einsum(layout, cos_table, imag_part, precision=highest)
    sin_real = jnp.einsum(layout, sin_table, real_part, precision=highest)
    sin_imag = jnp.einsum(layout, sin_table, imag_part, precision=highest)
    return (cos_real - orientation * sin_imag, cos_imag + orientation * sin_real)


def apply_twist(cos_table, sin_table, real_part, imag_part, orientation):
    return (
        cos_table * real_part - orientation * sin_table * imag_part,
        cos_table * imag_part + orientation * sin_table * real_part,
    )


def count_ids(count):
    return jnp.arange(count, dtype=jnp.int32)


def block_table(base_tables, freq_ids, offset, recorded_readings):
    base_cos, base_sin = base_tables
    shift_cos, shift_sin = angle_lookup(freq_ids, jnp.reshape(offset, (1,)), recorded_readings)
    cos_table = base_cos * shift_cos - base_sin * shift_sin
    sin_table = base_sin * shift_cos + base_cos * shift_sin
    return jnp.stack([cos_table, -sin_table]).astype(jnp.bfloat16)


def temporal_spectrum(waveforms, base_tables, layout, output_dims):
    recorded_readings = waveforms.shape[1]
    block_width = recorded_readings // time_blocks
    freq_ids = count_ids(base_tables[0].shape[0])

    def temporal_advance(running, block_id):
        offset = block_id * block_width
        dft_table = block_table(base_tables, freq_ids, offset, recorded_readings)
        segment = lax.dynamic_slice_in_dim(waveforms, offset, block_width, 1)
        return (
            running + jnp.einsum(layout, dft_table, segment, preferred_element_type=jnp.float32),
            None,
        )

    spectrum, _ = lax.scan(
        temporal_advance, jnp.zeros(output_dims, jnp.float32), count_ids(time_blocks)
    )
    return spectrum.astype(jnp.bfloat16)


def frequency_filter(local_spectrum, band_edges):
    values = local_spectrum.astype(jnp.float32)
    bin_count, full_count = (values.shape[1], values.shape[2])
    devices = lax.axis_size("chan")
    block_width = full_count // devices
    real_part = values[0].reshape(bin_count, devices, block_width)
    imag_part = values[1].reshape(bin_count, devices, block_width)
    cos_parts, sine_components = angle_lookup(count_ids(devices), count_ids(devices), devices)
    cos_width, sin_width = angle_lookup(count_ids(block_width), count_ids(block_width), block_width)
    cos_twist, sin_twist = angle_lookup(count_ids(devices), count_ids(block_width), full_count)
    real_part, imag_part = rotate(
        "kp,fpm->fkm", cos_parts, sine_components, real_part, imag_part, -1.0
    )
    real_part, imag_part = apply_twist(cos_twist, sin_twist, real_part, imag_part, -1.0)
    real_part, imag_part = rotate("mn,fkm->fkn", cos_width, sin_width, real_part, imag_part, -1.0)
    wave_ids = count_ids(devices)[:, None] + devices * count_ids(block_width)[None, :]
    magnitude = jnp.where(wave_ids > full_count // 2, full_count - wave_ids, wave_ids)[None]
    passing = (magnitude >= band_edges[0][:, None, None]) & (
        magnitude <= band_edges[1][:, None, None]
    )
    real_part = jnp.where(passing, real_part, 0.0)
    imag_part = jnp.where(passing, imag_part, 0.0)
    real_part, imag_part = rotate("mn,fkn->fkm", cos_width, sin_width, real_part, imag_part, 1.0)
    real_part, imag_part = apply_twist(cos_twist, sin_twist, real_part, imag_part, 1.0)
    real_part, imag_part = rotate(
        "kp,fkm->fpm", cos_parts, sine_components, real_part, imag_part, 1.0
    )
    restored = jnp.stack([real_part, imag_part]).reshape(2, bin_count, full_count) * (
        1.0 / full_count
    )
    return restored.astype(jnp.bfloat16)


def coefficient_spectra(basis, filtered, layout, frequencies, recorded_readings):
    basis_rank, channels, tap_count = basis.shape
    cos_table, sin_table = angle_lookup(
        count_ids(frequencies), count_ids(tap_count), recorded_readings
    )
    dft_table = jnp.stack([cos_table, -sin_table]).astype(jnp.bfloat16)
    filtered_real = filtered[0].astype(jnp.float32)
    filtered_imag = filtered[1].astype(jnp.float32)
    contract = "kfm," + layout + "->kf"
    basis_group = basis.reshape(basis_blocks, basis_rank // basis_blocks, channels, tap_count)

    def project(members):
        transformed = jnp.einsum(
            "kml,rfl->krfm", members, dft_table, preferred_element_type=jnp.float32
        )
        trans_real, trans_imag = (transformed[:, 0], transformed[:, 1])
        spectra_real = jnp.einsum(
            contract, trans_real, filtered_real, precision=highest
        ) + jnp.einsum(contract, trans_imag, filtered_imag, precision=highest)
        fourier_quadrature = jnp.einsum(
            contract, trans_real, filtered_imag, precision=highest
        ) - jnp.einsum(contract, trans_imag, filtered_real, precision=highest)
        return jnp.stack([spectra_real, fourier_quadrature], axis=1)

    return lax.map(project, basis_group).reshape(basis_rank, 2, frequencies)


def channel_power(filtered, base_tables, layout, frequencies, recorded_readings):
    freq_ids = count_ids(frequencies)
    weights = jnp.where(freq_ids == 0, 1.0, 2.0).astype(jnp.bfloat16)
    weighted = filtered * weights[None, :, None]
    block_width = recorded_readings // time_blocks
    contract = "r" + layout + ",rft->mt"

    def channel_advance(running, block_id):
        offset = block_id * block_width
        dft_table = block_table(base_tables, freq_ids, offset, recorded_readings)
        traces = jnp.einsum(contract, weighted, dft_table, preferred_element_type=jnp.float32) * (
            1.0 / recorded_readings
        )
        return (running, jnp.sum(traces * traces, axis=0))

    _, pieces = lax.scan(channel_advance, jnp.zeros((), jnp.float32), count_ids(time_blocks))
    return pieces.reshape(recorded_readings)


def local(waveforms, basis, bounds):
    devices = lax.axis_size("chan")
    position = lax.axis_index("chan")
    channels, recorded_readings = waveforms.shape
    basis_rank, _, tap_count = basis.shape
    frequencies = bounds.shape[1]
    full_count = channels * devices
    freq_ids = count_ids(frequencies)
    base_tables = angle_lookup(
        freq_ids, count_ids(recorded_readings // time_blocks), recorded_readings
    )
    layout = "fm"
    spectrum = temporal_spectrum(waveforms, base_tables, "rft,mt->rfm", (2, frequencies, channels))
    local_spectrum = lax.all_to_all(spectrum, "chan", split_axis=1, concat_axis=2, tiled=True)
    bin_count = local_spectrum.shape[1]
    band_edges = lax.dynamic_slice_in_dim(bounds, position * bin_count, bin_count, 1)
    filtered = lax.all_to_all(
        frequency_filter(local_spectrum, band_edges),
        "chan",
        split_axis=2,
        concat_axis=1,
        tiled=True,
    )
    spectra = coefficient_spectra(basis, filtered, layout, frequencies, recorded_readings)
    flattened = basis.reshape(basis_rank, channels * tap_count)
    gram_matrix = jnp.einsum("ka,ja->kj", flattened, flattened, preferred_element_type=jnp.float32)
    trace_power = channel_power(filtered, base_tables, layout, frequencies, recorded_readings)
    spectra, gram_matrix, trace_power = lax.psum((spectra, gram_matrix, trace_power), "chan")
    lag_count = recorded_readings // devices
    lag_start = position * lag_count
    cos_lags, sin_lags = angle_lookup(freq_ids, lag_start + count_ids(lag_count), recorded_readings)
    weights = jnp.where(freq_ids == 0, 1.0, 2.0).astype(jnp.float32)
    scaled_inphase = spectra[:, 0] * weights[None, :]
    weighted_imag = spectra[:, 1] * weights[None, :]
    correlation = (
        jnp.dot(scaled_inphase, cos_lags, precision=highest)
        - jnp.dot(weighted_imag, sin_lags, precision=highest)
    ) * (1.0 / recorded_readings)
    extended = jnp.concatenate([trace_power, trace_power[:tap_count]])
    running = jnp.concatenate([jnp.zeros((1,), jnp.float32), jnp.cumsum(extended)])
    energy = lax.dynamic_slice_in_dim(
        running, lag_start + tap_count, lag_count, 0
    ) - lax.dynamic_slice_in_dim(running, lag_start, lag_count, 0)
    energy_threshold = energy / (full_count * tap_count) + 1e-06
    cholesky_factor = jnp.linalg.cholesky(gram_matrix)
    solved = jax.scipy.linalg.cho_solve((cholesky_factor, True), correlation)
    detection = jnp.sum(correlation * solved, axis=0) / (basis_rank * energy_threshold)
    coefficients = correlation / jnp.sqrt(energy_threshold)[None, :]
    return (detection, coefficients)


def solution(mesh):
    in_specs = (P("chan", "groups"), P(None, "chan", None), P())
    out_specs = (P(("groups", "chan")), P(None, ("groups", "chan")))
    return jax.shard_map(local, mesh=mesh, in_specs=in_specs, out_specs=out_specs, check_vma=False)
```

profile of v0, /device:TPU:0, one launch (start us, length us, event | category | flops | bytes accessed | tf_op | source)
XLA Modules:
  0.0 827.4 jit_solution(9234787007890897605)
XLA Ops:
  7.2 148.7 %while.40 = (s32[]{:T(128)}, f32[2,768,640]{2,1,0:T(8,128)}, s32[4]{0:T(128)S(1)}, bf16[640,7680]{1,0:T(8,128)(2,1)}, s32[]{:T(128)}, /*index=5*/s32[]{:T(128)}, s32[1]{0:T(128)}, s32[]{:T(128)}) while((s32[]{:T(128)}, f32[2,768,640]{2,1,0:T(8,128)}, s32[4]{0:T(128)S(1)}, bf16[640,7680]{1,0:T(8,128)(2,1)}, s32[]{:T(128)}, ...), condition=%wide.region_1.2_spmd.clone.clone, body=%wide.region_0.1_spmd.clone.clone.sunk | while | flops 3806337792 | bytes 53588192 | solution.py:61
  8.5 25.9 %fusion.331 = (bf16[1,768,1920]{2,1,0:T(8,128)(2,1)S(1)}, bf16[1,768,1920]{2,1,0:T(8,128)(2,1)S(1)}) fusion(f32[768]{0:T(1024)S(1)} %get-tuple-element.499, f32[768]{0:T(1024)S(1)} %get-tuple-element.500), kind=kLoop, calls=%fused_computation.52.clone.1 | loop fusion | flops 26542080 | bytes 5904384 | tf_op jit(solution)/shard_map/convert
  34.5 8.1 select_add_fusion.2
  45.7 25.9 %fusion.331 = (bf16[1,768,1920]{2,1,0:T(8,128)(2,1)S(1)}, bf16[1,768,1920]{2,1,0:T(8,128)(2,1)S(1)}) fusion(f32[768]{0:T(1024)S(1)} %get-tuple-element.499, f32[768]{0:T(1024)S(1)} %get-tuple-element.500), kind=kLoop, calls=%fused_computation.52.clone.1 | loop fusion | flops 26542080 | bytes 5904384 | tf_op jit(solution)/shard_map/convert
  71.6 8.0 select_add_fusion.2
  82.9 25.9 %fusion.331 = (bf16[1,768,1920]{2,1,0:T(8,128)(2,1)S(1)}, bf16[1,768,1920]{2,1,0:T(8,128)(2,1)S(1)}) fusion(f32[768]{0:T(1024)S(1)} %get-tuple-element.499, f32[768]{0:T(1024)S(1)} %get-tuple-element.500), kind=kLoop, calls=%fused_computation.52.clone.1 | loop fusion | flops 26542080 | bytes 5904384 | tf_op jit(solution)/shard_map/convert
  108.8 8.1 select_add_fusion.2
  120.1 25.9 %fusion.331 = (bf16[1,768,1920]{2,1,0:T(8,128)(2,1)S(1)}, bf16[1,768,1920]{2,1,0:T(8,128)(2,1)S(1)}) fusion(f32[768]{0:T(1024)S(1)} %get-tuple-element.499, f32[768]{0:T(1024)S(1)} %get-tuple-element.500), kind=kLoop, calls=%fused_computation.52.clone.1 | loop fusion | flops 26542080 | bytes 5904384 | tf_op jit(solution)/shard_map/convert
  146.0 8.0 select_add_fusion.2
  155.9 6.4 copy.169
  162.4 7.6 all-to-all-start
  170.5 38.0 %all-to-all-done = bf16[2,768,640]{2,0,1:T(2,128)(2,1)S(1)} async-done(((bf16[2,768,640]{2,0,1:T(2,128)(2,1)}), bf16[2,768,640]{2,0,1:T(2,128)(2,1)S(1)}, u32[]{:S(2)}, u32[]{:S(2)}) %all-to-all-start) | async-done | bytes 1966112 | tf_op jit(solution)/shard_map/all_to_all | solution.py:159
  213.6 11.9 %fusion.89 = f32[48,16,640]{2,1,0:T(8,128)S(1)} fusion(f32[48,640,16]{1,2,0:T(8,128)S(1)} %multiply_add_fusion.1, f32[48,640,16]{1,2,0:T(8,128)S(1)} %multiply_subtract_fusion.1, f32[16,640]{1,0:T(8,128)S(1)} %get-tuple-element.385, f32[16,640]{1,0:T(8,128)S(1)} %get-tuple-element.384), kind=kOutput, calls=%fused_computation.124 | convolution fusion | flops 3780034560 | bytes 5980160 | tf_op jit(solution)/shard_map/mn,fkm->fkn/dot_general | solution.py:23
  225.5 11.7 %fusion.91 = f32[48,16,640]{2,1,0:T(8,128)S(1)} fusion(f32[48,640,16]{1,2,0:T(8,128)S(1)} %multiply_add_fusion.1, f32[48,640,16]{1,2,0:T(8,128)S(1)} %multiply_subtract_fusion.1, f32[16,640]{1,0:T(8,128)S(1)} %get-tuple-element.385, f32[16,640]{1,0:T(8,128)S(1)} %get-tuple-element.384), kind=kOutput, calls=%fused_computation.126 | convolution fusion | flops 3780034560 | bytes 5980160 | tf_op jit(solution)/shard_map/mn,fkm->fkn/dot_general | solution.py:24
  237.3 11.8 %add_select_fusion.6 = f32[48,16,640]{2,1,0:T(8,128)S(1)} fusion(f32[48,16,640]{2,1,0:T(8,128)S(1)} %fusion.89, s32[16,640]{1,0:T(8,128)S(1)} %compare_select_fusion, s32[48]{0:T(128)S(1)} %get-tuple-element.381, s32[48]{0:T(128)S(1)} %get-tuple-element.380, f32[48,640,16]{1,2,0:T(8,128)S(1)} %multiply_add_fusion.1, ...), kind=kOutput, calls=%fused_computation.113 | convolution fusion | flops 3782983680 | bytes 7987584 | tf_op jit(solution)/shard_map/mn,fkm->fkn/dot_general | solution.py:22
  249.0 11.8 %fusion.87 = f32[48,16,640]{2,1,0:T(8,128)S(1)} fusion(f32[48,16,640]{2,1,0:T(8,128)S(1)} %add_select_fusion.6), kind=kOutput, calls=%fused_computation.122 | convolution fusion | flops 3778560000 | bytes 3932160 | tf_op jit(solution)/shard_map/mn,fkn->fkm/dot_general | solution.py:24
  260.9 11.7 %subtract_select_fusion = f32[48,16,640]{2,1,0:T(8,128)S(1)} fusion(f32[48,16,640]{2,1,0:T(8,128)S(1)} %fusion.91, s32[16,640]{1,0:T(8,128)S(1)} %compare_select_fusion, s32[48]{0:T(128)S(1)} %get-tuple-element.381, s32[48]{0:T(128)S(1)} %get-tuple-element.380, f32[48,640,16]{1,2,0:T(8,128)S(1)} %multiply_add_fusion.1, ...), kind=kOutput, calls=%fused_computation.114 | convolution fusion | flops 3782983680 | bytes 7987584 | tf_op jit(solution)/shard_map/mn,fkm->fkn/dot_general | solution.py:21
  272.6 11.6 %fusion.85 = f32[48,16,640]{2,1,0:T(8,128)S(1)} fusion(f32[48,16,640]{2,1,0:T(8,128)S(1)} %subtract_select_fusion), kind=kOutput, calls=%fused_computation.120 | convolution fusion | flops 3778560000 | bytes 3932160 | tf_op jit(solution)/shard_map/mn,fkn->fkm/dot_general | solution.py:23
  284.2 11.9 %fusion.114 = f32[48,16,640]{2,1,0:T(8,128)S(1)} fusion(f32[48,16,640]{2,1,0:T(8,128)S(1)} %fusion.87, f32[48,16,640]{2,1,0:T(8,128)S(1)} %subtract_select_fusion), kind=kOutput, calls=%fused_computation.142 | convolution fusion | flops 3779051520 | bytes 5898240 | tf_op jit(solution)/shard_map/mn,fkn->fkm/dot_general | solution.py:21
  296.2 11.5 %fusion.117 = f32[48,16,640]{2,1,0:T(8,128)S(1)} fusion(f32[48,16,640]{2,1,0:T(8,128)S(1)} %fusion.85, f32[48,16,640]{2,1,0:T(8,128)S(1)} %add_select_fusion.6), kind=kOutput, calls=%fused_computation.143 | convolution fusion | flops 3779051520 | bytes 5898240 | tf_op jit(solution)/shard_map/mn,fkn->fkm/dot_general | solution.py:22
  307.7 2.0 fusion.185
  309.8 3.3 fusion.184
  313.1 3.3 add_bitcast_fusion.1
  316.4 2.8 stack.44
  319.2 5.5 subtract_bitcast_fusion.1
  324.7 2.9 stack.43
  327.6 3.4 fusion.80
  331.0 11.3 %copy.99 = bf16[2,48,10240]{1,0,2:T(2,128)(2,1)} copy(bf16[2,48,10240]{2,1,0:T(8,128)(2,1)} %fusion.80) | data formatting | bytes 3932160 | tf_op jit(solution)/shard_map/convert_element_type | solution.py:97
  342.2 10.5 %reshape.584 = bf16[16,2,30720]{2,1,0:T(2,128)(2,1)} reshape(bf16[10240,2,48]{2,1,0:T(2,128)(2,1)} %bitcast.263) | data formatting | bytes 3932160
  352.7 10.7 %all-to-all-start.1 = ((bf16[16,2,30720]{2,1,0:T(2,128)(2,1)}), bf16[16,2,30720]{2,1,0:T(2,128)(2,1)S(1)}, u32[]{:S(2)}, u32[]{:S(2)}) async-start(bf16[16,2,30720]{2,1,0:T(2,128)(2,1)} %reshape.584), calls=%async_computation.1 | async-start | bytes 3932160 | tf_op jit(solution)/shard_map/all_to_all | solution.py:162
  363.5 2.6 negate_convert_fusion
  366.2 5.1 fusion.142
  371.3 30.8 %all-to-all-done.1 = bf16[16,2,30720]{2,1,0:T(2,128)(2,1)S(1)} async-done(((bf16[16,2,30720]{2,1,0:T(2,128)(2,1)}), bf16[16,2,30720]{2,1,0:T(2,128)(2,1)S(1)}, u32[]{:S(2)}, u32[]{:S(2)}) %all-to-all-start.1) | async-done | bytes 1966112 | tf_op jit(solution)/shard_map/all_to_all | solution.py:162
  402.1 6.7 reshape.585
  408.8 9.6 %copy.148 = bf16[2,48,16,640]{3,1,2,0:T(8,128)(2,1)S(1)} copy(bf16[2,48,16,640]{1,0,3,2:T(2,128)(2,1)} %bitcast.261) | data formatting | bytes 3932160 | tf_op jit(solution)/shard_map/all_to_all | solution.py:162
  418.4 8.8 %copy.146 = bf16[2,48,16,640]{3,2,1,0:T(8,128)(2,1)} copy(bf16[2,48,16,640]{1,0,3,2:T(2,128)(2,1)} %bitcast.262) | data formatting | bytes 3932160 | tf_op jit(solution)/shard_map/all_to_all | solution.py:162
  428.9 4.1 copy.109
  433.0 126.7 %while.39 = (s32[]{:T(128)}, f32[4,1920]{1,0:T(4,128)S(1)}, s32[4]{0:T(128)S(1)}, bf16[2,768,640]{1,2,0:T(8,128)(2,1)}, s32[]{:T(128)}, /*index=5*/s32[1]{0:T(128)}, s32[]{:T(128)}) while((s32[]{:T(128)}, f32[4,1920]{1,0:T(4,128)S(1)}, s32[4]{0:T(128)S(1)}, bf16[2,768,640]{1,2,0:T(8,128)(2,1)}, s32[]{:T(128)}, ...), condition=%wide.region_11.12_spmd.clone.clone, body=%wide.region_9.11_spmd.clone.clone.sunk | while | flops 3808056064 | bytes 21677712 | solution.py:142
  434.3 25.9 %fusion.326 = (bf16[1,768,1920]{2,1,0:T(8,128)(2,1)S(1)}, bf16[1,768,1920]{2,1,0:T(8,128)(2,1)S(1)}) fusion(f32[768]{0:T(1024)S(1)} %get-tuple-element.491, f32[768]{0:T(1024)S(1)} %get-tuple-element.492), kind=kLoop, calls=%fused_computation.16.clone.1 | loop fusion | flops 26542080 | bytes 5904384 | tf_op jit(solution)/shard_map/convert.2
  460.3 4.3 fusion.327
  466.0 25.9 %fusion.326 = (bf16[1,768,1920]{2,1,0:T(8,128)(2,1)S(1)}, bf16[1,768,1920]{2,1,0:T(8,128)(2,1)S(1)}) fusion(f32[768]{0:T(1024)S(1)} %get-tuple-element.491, f32[768]{0:T(1024)S(1)} %get-tuple-element.492), kind=kLoop, calls=%fused_computation.16.clone.1 | loop fusion | flops 26542080 | bytes 5904384 | tf_op jit(solution)/shard_map/convert.2
  491.9 4.3 fusion.327
  497.7 25.9 %fusion.326 = (bf16[1,768,1920]{2,1,0:T(8,128)(2,1)S(1)}, bf16[1,768,1920]{2,1,0:T(8,128)(2,1)S(1)}) fusion(f32[768]{0:T(1024)S(1)} %get-tuple-element.491, f32[768]{0:T(1024)S(1)} %get-tuple-element.492), kind=kLoop, calls=%fused_computation.16.clone.1 | loop fusion | flops 26542080 | bytes 5904384 | tf_op jit(solution)/shard_map/convert.2
  523.6 4.3 fusion.327
  529.3 25.9 %fusion.326 = (bf16[1,768,1920]{2,1,0:T(8,128)(2,1)S(1)}, bf16[1,768,1920]{2,1,0:T(8,128)(2,1)S(1)}) fusion(f32[768]{0:T(1024)S(1)} %get-tuple-element.491, f32[768]{0:T(1024)S(1)} %get-tuple-element.492), kind=kLoop, calls=%fused_computation.16.clone.1 | loop fusion | flops 26542080 | bytes 5904384 | tf_op jit(solution)/shard_map/convert.2
  555.3 4.3 fusion.327
  559.7 67.2 %all-reduce.1 = (f32[16,16]{0,1:T(8,128)S(1)}, f32[7680]{0:T(1024)S(1)}) all-reduce(f32[16,16]{0,1:T(8,128)S(1)} %fusion.142, f32[7680]{0:T(1024)S(1)} %reshape.545), channel_id=1, replica_groups=mesh['groups'=2,'chan'=16] {'chan'}, use_global_device_ids=true, to_apply=%region_5.6 | all-reduce | flops 7936 | bytes 63488 | tf_op jit(solution)/shard_map/psum | solution.py:173
  629.8 1.9 copy.102
  631.7 84.8 %while.38 = (s32[]{:T(128)}, f32[4,4,2,768]{3,2,1,0:T(2,128)S(1)}, bf16[4,4,640,200]{2,3,1,0:T(8,128)(2,1)}, bf16[2,768,200]{1,2,0:T(8,128)(2,1)S(1)}, f32[768,640]{1,0:T(8,128)}, /*index=5*/f32[768,640]{1,0:T(8,128)}, s32[]{:T(128)}) while((s32[]{:T(128)}, f32[4,4,2,768]{3,2,1,0:T(2,128)S(1)}, bf16[4,4,640,200]{2,3,1,0:T(8,128)(2,1)}, ...), condition=%wide.region_3.4_spmd, body=%wide.region_2.3_spmd.sunk | while | flops 1588592640 | bytes 45113436 | solution.py:124
  631.7 9.1 %convolution_bitcast_fusion.2 = f32[4,2,768,640]{2,3,1,0:T(8,128)} fusion(bf16[4,4,640,200]{2,3,1,0:T(8,128)(2,1)} %get-tuple-element.564, s32[]{:T(128)S(6)} %copy.193, bf16[2,768,200]{1,2,0:T(8,128)(2,1)S(1)} %get-tuple-element.565), kind=kOutput, calls=%fused_computation.79.clone.1 | convolution fusion | flops 1572864000 | bytes 17367044 | tf_op jit(solution)/shard_map/while/body/eval_jaxpr/kml,rfl->krfm/dot_general | solution.py:112
  642.6 2.9 copy.176
  645.6 7.2 multiply_reduce_fusion.5
  652.9 9.1 %convolution_bitcast_fusion.2 = f32[4,2,768,640]{2,3,1,0:T(8,128)} fusion(bf16[4,4,640,200]{2,3,1,0:T(8,128)(2,1)} %get-tuple-element.564, s32[]{:T(128)S(6)} %copy.193, bf16[2,768,200]{1,2,0:T(8,128)(2,1)S(1)} %get-tuple-element.565), kind=kOutput, calls=%fused_computation.79.clone.1 | convolution fusion | flops 1572864000 | bytes 17367044 | tf_op jit(solution)/shard_map/while/body/eval_jaxpr/kml,rfl->krfm/dot_general | solution.py:112
  663.8 2.9 copy.176
  666.8 7.2 multiply_reduce_fusion.5
  674.1 9.1 %convolution_bitcast_fusion.2 = f32[4,2,768,640]{2,3,1,0:T(8,128)} fusion(bf16[4,4,640,200]{2,3,1,0:T(8,128)(2,1)} %get-tuple-element.564, s32[]{:T(128)S(6)} %copy.193, bf16[2,768,200]{1,2,0:T(8,128)(2,1)S(1)} %get-tuple-element.565), kind=kOutput, calls=%fused_computation.79.clone.1 | convolution fusion | flops 1572864000 | bytes 17367044 | tf_op jit(solution)/shard_map/while/body/eval_jaxpr/kml,rfl->krfm/dot_general | solution.py:112
  685.0 2.9 copy.176
  688.0 7.2 multiply_reduce_fusion.5
  695.3 9.1 %convolution_bitcast_fusion.2 = f32[4,2,768,640]{2,3,1,0:T(8,128)} fusion(bf16[4,4,640,200]{2,3,1,0:T(8,128)(2,1)} %get-tuple-element.564, s32[]{:T(128)S(6)} %copy.193, bf16[2,768,200]{1,2,0:T(8,128)(2,1)S(1)} %get-tuple-element.565), kind=kOutput, calls=%fused_computation.79.clone.1 | convolution fusion | flops 1572864000 | bytes 17367044 | tf_op jit(solution)/shard_map/while/body/eval_jaxpr/kml,rfl->krfm/dot_general | solution.py:112
  706.2 2.9 copy.176
  709.2 7.2 multiply_reduce_fusion.5
  721.3 82.0 %all-reduce.4.cloned.1.call-done = f32[16,2,768]{2,1,0:T(2,128)} async-done(((f32[16,2,768]{2,1,0:T(2,128)}), f32[16,2,768]{2,1,0:T(2,128)}) %all-reduce.4.cloned.1.call-update) | async-done | bytes 98320 | tf_op jit(solution)/shard_map/psum | solution.py:173
  804.4 6.9 fusion.122
  811.3 7.7 broadcast_divide_fusion
  (125 shorter events, 38.3 us)
Async XLA Ops:
  7.2 162.8 %copy-start = (s32[2,768]{1,0:T(2,128)S(1)}, s32[2,768]{1,0:T(2,128)}, u32[]{:S(2)}) copy-start(s32[2,768]{1,0:T(2,128)} %param.11) | copy-start | bytes 18436
  8.5 25.9 %copy-start.5 = (f32[2,768,640]{2,1,0:T(8,128)S(1)}, f32[2,768,640]{2,1,0:T(8,128)}, u32[]{:S(2)}) copy-start(f32[2,768,640]{2,1,0:T(8,128)} %get-tuple-element.512) | copy-start | bytes 11796484 | tf_op jit(solution)/shard_map/while
  42.5 1.9 copy-start.6
  45.7 25.9 %copy-start.5 = (f32[2,768,640]{2,1,0:T(8,128)S(1)}, f32[2,768,640]{2,1,0:T(8,128)}, u32[]{:S(2)}) copy-start(f32[2,768,640]{2,1,0:T(8,128)} %get-tuple-element.512) | copy-start | bytes 11796484 | tf_op jit(solution)/shard_map/while
  79.7 1.9 copy-start.6
  82.9 25.9 %copy-start.5 = (f32[2,768,640]{2,1,0:T(8,128)S(1)}, f32[2,768,640]{2,1,0:T(8,128)}, u32[]{:S(2)}) copy-start(f32[2,768,640]{2,1,0:T(8,128)} %get-tuple-element.512) | copy-start | bytes 11796484 | tf_op jit(solution)/shard_map/while
  116.9 1.9 copy-start.6
  120.1 25.9 %copy-start.5 = (f32[2,768,640]{2,1,0:T(8,128)S(1)}, f32[2,768,640]{2,1,0:T(8,128)}, u32[]{:S(2)}) copy-start(f32[2,768,640]{2,1,0:T(8,128)} %get-tuple-element.512) | copy-start | bytes 11796484 | tf_op jit(solution)/shard_map/while
  154.1 1.9 copy-start.6
  162.4 46.1 %all-to-all-start = ((bf16[2,768,640]{2,0,1:T(2,128)(2,1)}), bf16[2,768,640]{2,0,1:T(2,128)(2,1)S(1)}, u32[]{:S(2)}, u32[]{:S(2)}) async-start(bf16[2,768,640]{2,0,1:T(2,128)(2,1)} %copy.169), calls=%async_computation | async-start | bytes 3932160 | tf_op jit(solution)/shard_map/all_to_all | solution.py:159
  307.7 5.4 copy-start.2
  324.7 2.9 copy-start.4
  352.7 49.4 %all-to-all-start.1 = ((bf16[16,2,30720]{2,1,0:T(2,128)(2,1)}), bf16[16,2,30720]{2,1,0:T(2,128)(2,1)S(1)}, u32[]{:S(2)}, u32[]{:S(2)}) async-start(bf16[16,2,30720]{2,1,0:T(2,128)(2,1)} %reshape.584), calls=%async_computation.1 | async-start | bytes 3932160 | tf_op jit(solution)/shard_map/all_to_all | solution.py:162
  363.4 439.9 %all-reduce.4.cloned.1.call-start = ((), (), s32[]{:S(2)}) async-start(), calls=%async_computation.2 | async-start | bytes 196608 | tf_op jit(solution)/shard_map/psum | solution.py:173
  433.0 194.6 %copy-start.3 = (bf16[2,48,16,640]{3,2,1,0:T(8,128)(2,1)S(1)}, bf16[2,48,16,640]{3,2,1,0:T(8,128)(2,1)}, u32[]{:S(2)}) copy-start(bf16[2,48,16,640]{3,2,1,0:T(8,128)(2,1)} %copy.146) | copy-start | bytes 5898244
  434.3 25.9 %copy-start.7 = (bf16[2,768,640]{1,2,0:T(8,128)(2,1)S(1)}, bf16[2,768,640]{1,2,0:T(8,128)(2,1)}, u32[]{:S(2)}) copy-start(bf16[2,768,640]{1,2,0:T(8,128)(2,1)} %get-tuple-element.544) | copy-start | bytes 5898244 | tf_op jit(solution)/shard_map/while
  466.0 25.9 %copy-start.7 = (bf16[2,768,640]{1,2,0:T(8,128)(2,1)S(1)}, bf16[2,768,640]{1,2,0:T(8,128)(2,1)}, u32[]{:S(2)}) copy-start(bf16[2,768,640]{1,2,0:T(8,128)(2,1)} %get-tuple-element.544) | copy-start | bytes 5898244 | tf_op jit(solution)/shard_map/while
  497.7 25.9 %copy-start.7 = (bf16[2,768,640]{1,2,0:T(8,128)(2,1)S(1)}, bf16[2,768,640]{1,2,0:T(8,128)(2,1)}, u32[]{:S(2)}) copy-start(bf16[2,768,640]{1,2,0:T(8,128)(2,1)} %get-tuple-element.544) | copy-start | bytes 5898244 | tf_op jit(solution)/shard_map/while
  529.3 25.9 %copy-start.7 = (bf16[2,768,640]{1,2,0:T(8,128)(2,1)S(1)}, bf16[2,768,640]{1,2,0:T(8,128)(2,1)}, u32[]{:S(2)}) copy-start(bf16[2,768,640]{1,2,0:T(8,128)(2,1)} %get-tuple-element.544) | copy-start | bytes 5898244 | tf_op jit(solution)/shard_map/while
  716.5 0.6 copy-start.8
  811.3 8.7 %copy-start.1 = (s32[2,768]{1,0:T(2,128)S(1)}, s32[2,768]{1,0:T(2,128)}, u32[]{:S(2)}) copy-start(s32[2,768]{1,0:T(2,128)} %param.11) | copy-start | bytes 18436
Sparse Core Ops, SparseCore 0:
  717.3 86.0 all-reduce.3
where the time goes:
time: 837 us; the launch traced here: 827 us
  other arithmetic  250 us (30%)
  matrix products  218 us (26%)
  waiting for transfers between devices  151 us (18%)
  local copies, waits for them, and re-layouts  102 us (12%)
  blocking collectives  67.2 us (8%)
  starting transfers between devices  18.4 us (2%)
  between operations  14.9 us (2%)
    another operation x13, other arithmetic  210 us
    psum x1, waiting for transfers between devices, local(): lax.psum((spectra, gram_matrix, trace_power), 'chan')  82 us
    psum x1, blocking collectives, local(): lax.psum((spectra, gram_matrix, trace_power), 'chan')  67.2 us
    all_to_all x1, waiting for transfers between devices, local(): lax.all_to_all(spectrum, 'chan', split_axis=1, concat_axis=2, tiled=True)  38 us
    dot_general x4, matrix products, project(): jnp.einsum('kml,rfl->krfm', members, dft_table, preferred_element_type=jn...  36.2 us
    dot_general x4, matrix products, temporal_advance(): jnp.einsum(layout, dft_table, segment, preferred_element_type=jnp.float32)  32.2 us
    all_to_all x1, waiting for transfers between devices, local(): lax.all_to_all(frequency_filter(local_spectrum, band_edges), 'chan', spli...  30.8 us
    dot_general x4, matrix products, rotate(): sin_imag = jnp.einsum(layout, sin_table, imag_part, precision=highest)  30.2 us
  transfers between devices with their start and end apart: 3, of which 3 were waited for; matrix products, arithmetic and copies ran while one was open for 2% of the time, Pallas kernels for 0%

commit v1 on v0

v1 whole, which is shorter than its diff:
```python
import functools
import math

import jax
import jax.numpy as jnp
import numpy as np
from jax import lax
from jax.experimental import pallas as pl
from jax.experimental.pallas import tpu as pltpu
from jax.sharding import PartitionSpec as P

radix = 12
half = radix // 2
lanes = 128
highest = lax.Precision.HIGHEST
bf16 = jnp.bfloat16
f32 = jnp.float32
vmem_limit = 60 * 1024 * 1024


def even_parts(x0, x6, s):
    r = math.sqrt(3.0) / 2.0
    s1, s2, s3, s4, s5 = s
    u, v = x0 + x6, x0 - x6
    e24, d24, e15, d15 = s2 + s4, s2 - s4, s1 + s5, s1 - s5
    even0, odd0 = u + e24, e15 + s3
    even1, odd1 = v + 0.5 * d24, r * d15
    even2, odd2 = u - 0.5 * e24, 0.5 * e15 - s3
    return (
        even0 + odd0,
        even1 + odd1,
        even2 + odd2,
        v - d24,
        even2 - odd2,
        even1 - odd1,
        even0 - odd0,
    )


def odd_parts(d):
    r = math.sqrt(3.0) / 2.0
    d1, d2, d3, d4, d5 = d
    e15, m15 = d1 + d5, d1 - d5
    odd1, even1 = 0.5 * e15 + d3, r * (d2 + d4)
    odd2, even2 = r * m15, r * (d2 - d4)
    return (odd1 + even1, odd2 + even2, e15 - d3, odd2 - even2, odd1 - even1)


def bin_order(frequencies):
    ids = np.arange(frequencies)
    groups = [np.concatenate([ids[ids % radix == 0], ids[ids % radix == half]])]
    signs = [np.ones(frequencies // half)]
    for q in range(1, half):
        plus, minus = ids[ids % radix == q], ids[ids % radix == radix - q]
        groups.append(np.concatenate([plus, minus]))
        signs.append(np.concatenate([np.ones(len(plus)), -np.ones(len(minus))]))
    return np.stack(groups), np.stack(signs)


def time_table(frequencies, readings, fold):
    width = readings // radix
    groups, signs = bin_order(frequencies)
    theta = (groups[:, :, None] * np.arange(width)[None, None, :] % readings) * (
        2.0 * np.pi / readings
    )
    cos, sin = np.cos(theta), np.sin(theta)
    sg = signs[:, :, None]
    real = np.concatenate([cos, -sg * sin], axis=2)
    imag = np.concatenate([-sin, -sg * cos], axis=2)
    first = (groups[0] % radix == 0)[:, None]
    real[0] = np.concatenate([np.where(first, cos[0], 0), np.where(first, 0, cos[0])], axis=1)
    imag[0] = np.concatenate([np.where(first, -sin[0], 0), np.where(first, 0, -sin[0])], axis=1)
    count = groups.shape[1]
    both = np.stack([real, imag], axis=1).reshape(half, 2, count // fold, fold, 2 * width)
    return both.transpose(0, 2, 1, 3, 4).reshape(half, 2 * count, 2 * width)


def row_bins(frequencies, fold):
    order = bin_order(frequencies)[0].reshape(-1, 1, fold)
    return np.broadcast_to(order, (order.shape[0], 2, fold)).reshape(-1)


def spectrum_kernel(x_ref, table_ref, out_ref, y_ref):
    rows, readings = x_ref.shape
    width = readings // radix
    for r0 in range(0, rows, 16):
        rs = slice(r0, r0 + 16)
        for b0 in range(0, width, lanes):
            x = [
                x_ref[rs, a * width + b0 : a * width + b0 + lanes].astype(f32)
                for a in range(radix)
            ]
            yr = even_parts(x[0], x[half], [x[a] + x[radix - a] for a in range(1, half)])
            ys = odd_parts([x[a] - x[radix - a] for a in range(1, half)])
            left = slice(b0, b0 + lanes)
            right = slice(width + b0, width + b0 + lanes)
            y_ref[0, rs, left] = yr[0].astype(bf16)
            y_ref[0, rs, right] = yr[half].astype(bf16)
            for q in range(1, half):
                y_ref[q, rs, left] = yr[q].astype(bf16)
                y_ref[q, rs, right] = ys[q - 1].astype(bf16)
    count = table_ref.shape[1]
    for g in range(half):
        out_ref[g * count : (g + 1) * count, :] = lax.dot_general(
            table_ref[g], y_ref[g], (((1,), (1,)), ((), ())), preferred_element_type=f32
        ).astype(bf16)


def time_spectrum(waveforms, table):
    channels, readings = waveforms.shape
    block = lanes if channels % lanes == 0 else channels
    rows = table.shape[0] * table.shape[1]
    return pl.pallas_call(
        spectrum_kernel,
        out_shape=jax.ShapeDtypeStruct((rows, channels), bf16),
        grid=(channels // block,),
        in_specs=[
            pl.BlockSpec((block, readings), lambda i: (i, 0)),
            pl.BlockSpec(table.shape, lambda i: (0, 0, 0)),
        ],
        out_specs=pl.BlockSpec((rows, block), lambda i: (0, i)),
        scratch_shapes=[pltpu.VMEM((half, block, 2 * readings // radix), bf16)],
        compiler_params=pltpu.CompilerParams(vmem_limit_bytes=vmem_limit),
        name="time_spectrum",
    )(waveforms, table)


def power_kernel(f_ref, table_ref, out_ref, z_ref):
    rows = f_ref.shape[1]
    width = z_ref.shape[2] // 2
    count = table_ref.shape[1]

    @pl.when(pl.program_id(0) == 0)
    def _():
        out_ref[...] = jnp.zeros_like(out_ref)

    for g in range(half):
        z_ref[g] = lax.dot_general(
            f_ref[g * count : (g + 1) * count, :],
            table_ref[g],
            (((0,), (0,)), ((), ())),
            preferred_element_type=f32,
        )
    step = 16
    for b0 in range(0, width, lanes):
        left = slice(b0, b0 + lanes)
        right = slice(width + b0, width + b0 + lanes)
        for r0 in range(0, rows, step):
            rs = slice(r0, r0 + step)
            zr = [z_ref[g, rs, left] for g in range(half)]
            zs = [z_ref[g, rs, right] for g in range(half)]
            even = even_parts(zr[0], zs[0], zr[1:])
            odd = odd_parts(zs[1:])
            for a in range(radix):
                m = min(a, radix - a)
                value = even[m]
                if 0 < a < half:
                    value = value + odd[m - 1]
                if a > half:
                    value = value - odd[m - 1]
                square = value * value
                total = square[0:8]
                for s in range(8, step, 8):
                    total = total + square[s : s + 8]
                out_ref[a, :, left] += total


def time_power(filtered, table):
    rows, channels = filtered.shape
    block = lanes if channels % lanes == 0 else channels
    width = table.shape[2] // 2
    pieces = pl.pallas_call(
        power_kernel,
        out_shape=jax.ShapeDtypeStruct((radix, 8, width), f32),
        grid=(channels // block,),
        in_specs=[
            pl.BlockSpec((rows, block), lambda i: (0, i)),
            pl.BlockSpec(table.shape, lambda i: (0, 0, 0)),
        ],
        out_specs=pl.BlockSpec((radix, 8, width), lambda i: (0, 0, 0)),
        scratch_shapes=[pltpu.VMEM((half, block, 2 * width), f32)],
        compiler_params=pltpu.CompilerParams(vmem_limit_bytes=vmem_limit),
        name="time_power",
    )(filtered, table)
    return jnp.sum(pieces, axis=1).reshape(-1)


def filter_tables(full_count, block_count, parts):
    n2 = lanes
    n1 = full_count // n2
    order = np.arange(n1).reshape(block_count, parts).T.reshape(-1)
    k1, k2, j = np.arange(n1), np.arange(n2), np.arange(n2)
    a1 = 2.0 * np.pi * ((k1[:, None] * order[None, :]) % n1) / n1
    a2 = 2.0 * np.pi * ((j[:, None] * k2[None, :]) % n2) / n2
    at = 2.0 * np.pi * ((k1[:, None] * j[None, :]) % full_count) / full_count
    c1, s1, c2, s2 = np.cos(a1), np.sin(a1), np.cos(a2), np.sin(a2)
    first = np.block([[c1, s1], [-s1, c1]])
    second = np.block([[c2, -s2], [s2, c2]])
    twist = np.stack([np.cos(at), np.sin(at)])
    wave = k1[:, None] + n1 * k2[None, :]
    magnitude = np.minimum(wave, full_count - wave).astype(np.int32)
    return (
        jnp.asarray(first, bf16),
        jnp.asarray(second, bf16),
        jnp.asarray(first.T.copy(), bf16),
        jnp.asarray(second.T.copy(), bf16),
        jnp.asarray(twist, f32),
        jnp.asarray(magnitude),
    )


def filter_kernel(fold, edges_ref, scale_ref, x_ref, w1_ref, w2_ref, v1_ref, v2_ref, tw_ref, mag_ref, o_ref):
    step = pl.program_id(0)
    devices = x_ref.shape[0]
    parts = x_ref.shape[2] // lanes
    n1 = mag_ref.shape[0]
    pieces = []
    for ri in range(2):
        for p in range(parts):
            piece = x_ref[:, ri * fold : (ri + 1) * fold, p * lanes : (p + 1) * lanes]
            pieces.append(jnp.swapaxes(piece.astype(f32), 0, 1).astype(bf16))
    stacked = jnp.concatenate(
        [jnp.concatenate([piece[fi] for piece in pieces], axis=0) for fi in range(fold)], axis=1
    )
    waves = jnp.dot(w1_ref[...], stacked, preferred_element_type=f32)
    tc, ts = tw_ref[0], tw_ref[1]
    rows = []
    for fi in range(fold):
        col = slice(fi * lanes, (fi + 1) * lanes)
        re, im = waves[:n1, col], waves[n1:, col]
        rows.append(
            jnp.concatenate([re * tc + im * ts, im * tc - re * ts], axis=1).astype(bf16)
        )
    waves = jnp.dot(jnp.concatenate(rows, axis=0), w2_ref[...], preferred_element_type=f32)
    mag = mag_ref[...]
    rows = []
    for fi in range(fold):
        low, high = edges_ref[0, step * fold + fi], edges_ref[1, step * fold + fi]
        passing = (mag >= low) & (mag <= high)
        block = waves[fi * n1 : (fi + 1) * n1]
        rows.append(
            jnp.concatenate(
                [
                    jnp.where(passing, block[:, :lanes], 0.0),
                    jnp.where(passing, block[:, lanes:], 0.0),
                ],
                axis=1,
            ).astype(bf16)
        )
    waves = jnp.dot(jnp.concatenate(rows, axis=0), v2_ref[...], preferred_element_type=f32)
    cols = []
    for fi in range(fold):
        block = waves[fi * n1 : (fi + 1) * n1] * scale_ref[0, step * fold + fi]
        re, im = block[:, :lanes], block[:, lanes:]
        cols.append(
            jnp.concatenate([re * tc - im * ts, im * tc + re * ts], axis=0).astype(bf16)
        )
    out = jnp.dot(v1_ref[...], jnp.concatenate(cols, axis=1), preferred_element_type=f32)
    for ri in range(2):
        for p in range(parts):
            r0 = (ri * parts + p) * devices
            piece = jnp.stack(
                [out[r0 : r0 + devices, fi * lanes : (fi + 1) * lanes] for fi in range(fold)]
            )
            o_ref[:, ri * fold : (ri + 1) * fold, p * lanes : (p + 1) * lanes] = jnp.swapaxes(
                piece, 0, 1
            ).astype(bf16)


def filter_fused(gathered, edges, scale, fold):
    devices, rows, channels = gathered.shape
    tables = filter_tables(devices * channels, devices, channels // lanes)
    whole = [pl.BlockSpec(t.shape, lambda i, n=t.ndim: (0,) * n) for t in tables]
    block = pl.BlockSpec((devices, 2 * fold, channels), lambda i: (0, i, 0))
    smem = pl.BlockSpec(memory_space=pltpu.SMEM)
    return pl.pallas_call(
        functools.partial(filter_kernel, fold),
        out_shape=jax.ShapeDtypeStruct(gathered.shape, bf16),
        grid=(rows // (2 * fold),),
        in_specs=[smem, smem, block] + whole,
        out_specs=block,
        compiler_params=pltpu.CompilerParams(vmem_limit_bytes=vmem_limit),
        name="fan_filter",
    )(edges, scale, gathered, *tables)


def filter_plain(gathered, edges, scale, fold):
    devices, rows, channels = gathered.shape
    full_count = devices * channels
    values = gathered.reshape(devices, rows // (2 * fold), 2, fold, channels)
    values = values.transpose(2, 1, 3, 0, 4).reshape(2, rows // 2, devices, channels)
    d, m = np.arange(devices), np.arange(channels)
    ad = 2.0 * np.pi * (d[:, None] * d[None, :] % devices) / devices
    am = 2.0 * np.pi * (m[:, None] * m[None, :] % channels) / channels
    at = 2.0 * np.pi * (d[:, None] * m[None, :]) / full_count
    wave = d[:, None] + devices * m[None, :]
    magnitude = jnp.asarray(np.minimum(wave, full_count - wave), jnp.int32)[None]

    def turn(layout, angle, pair, sign):
        c, s = jnp.asarray(np.cos(angle), f32), jnp.asarray(sign * np.sin(angle), f32)
        ein = functools.partial(jnp.einsum, layout, precision=highest)
        return ein(c, pair[0]) - ein(s, pair[1]), ein(c, pair[1]) + ein(s, pair[0])

    def twist(pair, sign):
        c, s = jnp.asarray(np.cos(at), f32), jnp.asarray(sign * np.sin(at), f32)
        return c * pair[0] - s * pair[1], c * pair[1] + s * pair[0]

    pair = (values[0].astype(f32), values[1].astype(f32))
    pair = twist(turn("kp,fpm->fkm", ad, pair, -1.0), -1.0)
    pair = turn("mn,fkm->fkn", am, pair, -1.0)
    passing = (magnitude >= edges[0][:, None, None]) & (magnitude <= edges[1][:, None, None])
    pair = tuple(jnp.where(passing, part, 0.0) for part in pair)
    pair = twist(turn("mn,fkn->fkm", am, pair, 1.0), 1.0)
    pair = turn("kp,fkm->fpm", ad, pair, 1.0)
    out = (jnp.stack(pair) * scale[0][None, :, None, None]).astype(bf16)
    out = out.reshape(2, rows // (2 * fold), fold, devices, channels).transpose(3, 1, 0, 2, 4)
    return out.reshape(devices, rows, channels)


def coefficient_kernel(b_ref, f_ref, cos_ref, sin_ref, out_ref):
    sums = lax.dot_general(
        b_ref[0], f_ref[...], (((1,), (1,)), ((), ())), preferred_element_type=f32
    )
    out_ref[0, 0:1, :] = jnp.sum(sums * cos_ref[...], axis=0, keepdims=True)
    out_ref[0, 1:2, :] = jnp.sum(sums * sin_ref[...], axis=0, keepdims=True)


def coefficient_spectra(turned, filtered, readings, fold):
    rank, taps, channels = turned.shape
    rows = filtered.shape[0]
    bins = row_bins(rows // 2, fold)
    angle = 2.0 * np.pi * (np.arange(taps)[:, None] * bins[None, :] % readings) / readings
    whole = lambda i: (0, 0)
    products = pl.pallas_call(
        coefficient_kernel,
        out_shape=jax.ShapeDtypeStruct((rank, 2, rows), f32),
        grid=(rank,),
        in_specs=[
            pl.BlockSpec((1, taps, channels), lambda i: (i, 0, 0)),
            pl.BlockSpec(filtered.shape, whole),
            pl.BlockSpec(angle.shape, whole),
            pl.BlockSpec(angle.shape, whole),
        ],
        out_specs=pl.BlockSpec((1, 2, rows), lambda i: (i, 0, 0)),
        compiler_params=pltpu.CompilerParams(vmem_limit_bytes=vmem_limit),
        name="coefficient_spectra",
    )(turned, filtered, jnp.asarray(np.cos(angle), f32), jnp.asarray(np.sin(angle), f32))
    parts = products.reshape(rank, 2, rows // (2 * fold), 2, fold)
    real = parts[:, 0, :, 0] - parts[:, 1, :, 1]
    imag = parts[:, 1, :, 0] + parts[:, 0, :, 1]
    return jnp.stack([real, imag], axis=2).reshape(rank, rows)


def lag_series(spectra, table):
    rank = spectra.shape[0]
    count, width = table.shape[1], table.shape[2] // 2
    high = spectra.astype(bf16)
    low = (spectra - high.astype(f32)).astype(bf16)
    both = jnp.stack([high, low]).reshape(2 * rank, half, count)
    z = jnp.einsum("rgk,gkb->grb", both, table, preferred_element_type=f32)
    z = z[:, :rank] + z[:, rank:]
    zr, zs = z[:, :, :width], z[:, :, width:]
    even = even_parts(zr[0], zs[0], [zr[g] for g in range(1, half)])
    odd = odd_parts([zs[g] for g in range(1, half)])
    series = [even[0]]
    series += [even[a] + odd[a - 1] for a in range(1, half)]
    series += [even[half]]
    series += [even[a] - odd[a - 1] for a in range(half - 1, 0, -1)]
    return jnp.concatenate(series, axis=1)


def local(waveforms, basis, bounds):
    devices = lax.axis_size("chan")
    position = lax.axis_index("chan")
    channels, readings = waveforms.shape
    rank, _, taps = basis.shape
    frequencies = bounds.shape[1]
    full_count = channels * devices
    bin_count = frequencies // devices
    fold = math.gcd(16, bin_count)
    lag_count = readings // devices

    table = jnp.asarray(time_table(frequencies, readings, fold), bf16)
    spectrum = time_spectrum(waveforms, table)
    gathered = lax.all_to_all(spectrum, "chan", split_axis=0, concat_axis=0, tiled=True)

    flat = basis.reshape(rank, channels * taps)
    gram_part = jnp.einsum("ka,ja->kj", flat, flat, preferred_element_type=f32)
    gram = jnp.sum(lax.all_gather(gram_part, "chan"), axis=0)
    factor = jnp.linalg.cholesky(gram)
    inverse = jax.scipy.linalg.cho_solve((factor, True), jnp.eye(rank, dtype=f32))
    turned = jnp.swapaxes(basis, 1, 2)

    order = bin_order(frequencies)[0].reshape(-1)
    edges = lax.dynamic_slice_in_dim(bounds[:, order], position * bin_count, bin_count, 1)
    scale = jnp.asarray(np.where(order == 0, 0.5, 1.0) / full_count, f32).reshape(1, -1)
    scale = lax.dynamic_slice_in_dim(scale, position * bin_count, bin_count, 1)
    gathered = gathered.reshape(devices, 2 * bin_count, channels)
    apply = filter_fused if channels % lanes == 0 else filter_plain
    passed = apply(gathered, edges, scale, fold).reshape(2 * frequencies, channels)
    filtered = lax.all_to_all(passed, "chan", split_axis=0, concat_axis=0, tiled=True)

    power = time_power(filtered, table)
    extended = jnp.concatenate([power, power[:taps]])
    windows = jnp.stack(
        [extended[d * lag_count : (d + 1) * lag_count + taps] for d in range(devices)]
    )
    windows = jnp.sum(
        lax.all_to_all(windows, "chan", split_axis=0, concat_axis=0, tiled=True),
        axis=0,
        keepdims=True,
    )
    spectra = coefficient_spectra(turned, filtered, readings, fold)
    series = lag_series(spectra, table)
    series = series.reshape(rank, devices, lag_count).transpose(1, 0, 2)
    series = lax.all_to_all(series, "chan", split_axis=0, concat_axis=0, tiled=True)
    correlation = jnp.sum(series, axis=0) * (2.0 / readings)

    lag = np.arange(lag_count + taps)[:, None] - np.arange(lag_count)[None, :]
    band = jnp.asarray((lag >= 0) & (lag < taps), f32)
    energy = jnp.dot(windows, band, precision=highest)[0] * (2.0 / readings) ** 2
    level = energy / (full_count * taps) + 1e-06
    solved = jnp.dot(inverse, correlation, precision=highest)
    detection = jnp.sum(correlation * solved, axis=0) / (rank * level)
    coefficients = correlation / jnp.sqrt(level)[None, :]
    return (detection, coefficients)


def solution(mesh):
    in_specs = (P("chan", "groups"), P(None, "chan", None), P())
    out_specs = (P(("groups", "chan")), P(None, ("groups", "chan")))
    return jax.shard_map(local, mesh=mesh, in_specs=in_specs, out_specs=out_specs, check_vma=False)
```

time: 837 us -> 203 us (0.24); the launches traced: 827 us -> 202 us
  other arithmetic: 250 us -> 7.86 us
  matrix products: 218 us -> 9.2 us
  waiting for transfers between devices: 151 us -> 46.1 us
  local copies, waits for them, and re-layouts: 102 us -> 13.6 us
  Pallas kernels: 0 us -> 45.6 us
  blocking collectives: 67.2 us -> 43.7 us
  starting transfers between devices: 18.4 us -> 34.8 us
  between operations: 14.9 us -> 1.08 us
    another operation x19 -> x7, other arithmetic: 214 us -> 4.08 us  [the longest x3 2.13 us: local(): factor = jnp.linalg.cholesky(gram)]
    dot_general x31 -> x4, matrix products: 218 us -> 8.86 us  [the longest x1 5.1 us: local(): gram_part = jnp.einsum('ka,ja->kj', flat, flat, preferred_element_type=f32)]
    psum x1 -> x0, waiting for transfers between devices: 82 us -> none  [local(): lax.psum((spectra, gram_matrix, trace_power), 'chan')]
    psum x1 -> x0, blocking collectives: 67.2 us -> none  [local(): lax.psum((spectra, gram_matrix, trace_power), 'chan')]
    pallas_call x0 -> x4, Pallas kernels: none -> 45.6 us  [the longest x1 17.4 us: coefficient_spectra(): pl.pallas_call(coefficient_kernel, out_shape=jax.ShapeDtypeStruct((rank,...]
    all_gather x0 -> x1, blocking collectives: none -> 43.7 us  [local(): gram = jnp.sum(lax.all_gather(gram_part, 'chan'), axis=0)]
    while x33 -> x0, local copies, waits for them, and re-layouts: 33.1 us -> none
    dot_general x4 -> x0, other arithmetic: 28.8 us -> none  [project(): jnp.einsum(contract, trans_imag, filtered_imag, precision=highest)]
  transfers between devices with their start and end apart: 3 -> 4, of which waited for: 3 -> 2; matrix products, arithmetic and copies ran while one was open for 2% -> 12% of each run, Pallas kernels for 0% -> 9%
where the time goes in v1:
time: 203 us; the launch traced here: 202 us
  waiting for transfers between devices  46.1 us (23%)
  Pallas kernels  45.6 us (22%)
  blocking collectives  43.7 us (22%)
  starting transfers between devices  34.8 us (17%)
  local copies, waits for them, and re-layouts  13.6 us (7%)
  matrix products  9.2 us (5%)
  other arithmetic  7.86 us (4%)
    all_gather x1, blocking collectives, local(): gram = jnp.sum(lax.all_gather(gram_part, 'chan'), axis=0)  43.7 us
    all_to_all x1, waiting for transfers between devices, local(): lax.all_to_all(spectrum, 'chan', split_axis=0, concat_axis=0, tiled=True)  35 us
    pallas_call x1, Pallas kernels, coefficient_spectra(): pl.pallas_call(coefficient_kernel, out_shape=jax.ShapeDtypeStruct((rank,...  17.4 us
    pallas_call x1, Pallas kernels, time_spectrum(): pl.pallas_call(spectrum_kernel, out_shape=jax.ShapeDtypeStruct((rows, cha...  12.4 us
    all_to_all x1, waiting for transfers between devices, local(): lax.all_to_all(series, 'chan', split_axis=0, concat_axis=0, tiled=True)  11.2 us
    all_to_all x1, starting transfers between devices, local(): lax.all_to_all(passed, 'chan', split_axis=0, concat_axis=0, tiled=True)  10.7 us
    all_to_all x1, starting transfers between devices, local(): lax.all_to_all(windows, 'chan', split_axis=0, concat_axis=0, tiled=True)  10.6 us
    pallas_call x1, Pallas kernels, time_power(): pl.pallas_call(power_kernel, out_shape=jax.ShapeDtypeStruct((radix, 8, wi...  9.71 us
  transfers between devices with their start and end apart: 4, of which 2 were waited for; matrix products, arithmetic and copies ran while one was open for 12% of the time, Pallas kernels for 9%

profile of v1, /device:TPU:0, one launch (start us, length us, event | category | flops | bytes accessed | tf_op | source)
XLA Modules:
  0.0 202.0 jit_solution(6252737288803528195)
XLA Ops:
  0.6 12.4 %time_spectrum.1 = bf16[1536,640]{1,0:T(8,128)(2,1)} custom-call(bf16[640,7680]{1,0:T(8,128)(2,1)} %x_ref.1, bf16[6,256,1280]{2,1,0:T(8,128)(2,1)} %constant.102.clone.table_ref), custom_call_target="tpu_custom_call" | custom-call | tf_op jit(solution)/shard_map/time_spectrum/pallas_call | solution.py:113
  13.1 0.0 copy-start.3
  13.1 0.0 copy-start.4
  13.1 7.5 %all-to-all-start = ((bf16[16,96,640]{2,1,0:T(8,128)(2,1)}), bf16[16,96,640]{2,1,0:T(8,128)(2,1)S(1)}, u32[]{:S(2)}, u32[]{:S(2)}) async-start(bf16[16,96,640]{2,1,0:T(8,128)(2,1)} %bitcast.152), calls=%async_computation | async-start | bytes 3932160 | tf_op jit(solution)/shard_map/all_to_all | solution.py:385
  20.6 0.0 copy-done.3
  20.6 0.2 copy.46
  20.8 0.0 copy-done.4
  20.9 1.6 gather_fusion
  22.5 0.6 copy.57
  23.1 1.3 dynamic-slice_bitcast_fusion.scale_ref
  24.4 35.0 %all-to-all-done.x_ref = bf16[16,96,640]{2,1,0:T(8,128)(2,1)S(1)} async-done(((bf16[16,96,640]{2,1,0:T(8,128)(2,1)}), bf16[16,96,640]{2,1,0:T(8,128)(2,1)S(1)}, u32[]{:S(2)}, u32[]{:S(2)}) %all-to-all-start) | async-done | bytes 1966112 | tf_op jit(solution)/shard_map/all_to_all | solution.py:385
  59.3 0.0 copy-start.1
  59.3 1.3 copy-done.1
  60.6 6.0 %fan_filter.1 = bf16[16,96,640]{2,1,0:T(8,128)(2,1)} custom-call(s32[2,48]{1,0:T(2,128)} %bitcast.159, f32[1,48]{1,0:T(1,128)} %dynamic-slice_bitcast_fusion.scale_ref, bf16[16,96,640]{2,1,0:T(8,128)(2,1)} %copy-done.1, bf16[160,160]{1,0:T(8,128)(2,1)} %constant.106.clone.w1_ref, bf16[256,256]{1,0:T(8,128)(2,1)} %constant.107.clone.w2_ref, ...), custom_call_target="tpu_custom_call" | custom-call | tf_op jit(solution)/shard_map/fan_filter/pallas_call | solution.py:276
  66.6 10.7 %all-to-all-start.1 = ((bf16[16,96,640]{2,1,0:T(8,128)(2,1)}), bf16[16,96,640]{2,1,0:T(8,128)(2,1)S(1)}, u32[]{:S(2)}, u32[]{:S(2)}) async-start(bf16[16,96,640]{2,1,0:T(8,128)(2,1)} %fan_filter.1), calls=%async_computation.1 | async-start | bytes 3932160 | tf_op jit(solution)/shard_map/all_to_all | solution.py:401
  77.3 5.1 %fusion.3 = f32[16,16]{1,0:T(8,128)S(1)} fusion(bf16[16,640,200]{1,2,0:T(8,128)(2,1)} %param.17), kind=kOutput, calls=%fused_computation.5 | convolution fusion | flops 65536000 | bytes 4097024 | tf_op jit(solution)/shard_map/ka,ja->kj/dot_general | solution.py:388
  82.4 43.7 %all-gather = f32[256,16]{1,0:T(8,128)S(1)} all-gather(f32[16,16]{1,0:T(8,128)S(1)} %fusion.3), channel_id=2, replica_groups=mesh['groups'=2,'chan'=16] {'chan'}, dimensions={0}, use_global_device_ids=true | all-gather | bytes 17408 | tf_op jit(solution)/shard_map/all_gather | solution.py:389
  126.2 0.1 copy.56
  126.2 1.5 cholesky.17
  127.7 0.6 compare_reduce_fusion
  128.4 0.0 all-to-all-done.1
  128.4 0.0 copy-start
  128.4 1.3 copy-done
  129.7 9.7 %time_power.1 = f32[12,8,640]{2,1,0:T(8,128)} custom-call(bf16[1536,640]{1,0:T(8,128)(2,1)} %bitcast.150, bf16[6,256,1280]{2,1,0:T(8,128)(2,1)} %constant.102.clone.table_ref), custom_call_target="tpu_custom_call" | custom-call | tf_op jit(solution)/shard_map/time_power/pallas_call | solution.py:172
  139.4 1.0 reduce_sum.48
  140.4 0.1 pad_maximum_fusion.2
  140.7 0.1 stack.79
  140.8 0.6 all_to_all.25
  141.4 10.6 %all-to-all-start.3 = ((f32[16,1,680]{2,1,0:T(1,128)}), f32[16,1,680]{2,1,0:T(1,128)S(1)}, u32[]{:S(2)}, u32[]{:S(2)}) async-start(f32[16,1,680]{2,1,0:T(1,128)} %all_to_all.25), calls=%async_computation.3 | async-start | bytes 98304 | tf_op jit(solution)/shard_map/all_to_all | solution.py:409
  152.0 17.4 %coefficient_spectra.1 = f32[16,2,1536]{2,1,0:T(2,128)} custom-call(bf16[16,200,640]{2,1,0:T(8,128)(2,1)} %bitcast.153, bf16[1536,640]{1,0:T(8,128)(2,1)} %bitcast.151, f32[200,1536]{1,0:T(8,128)} %constant.112.clone.cos_ref, f32[200,1536]{1,0:T(8,128)} %constant.113.clone.sin_ref), custom_call_target="tpu_custom_call" | custom-call | tf_op jit(solution)/shard_map/coefficient_spectra/pallas_call | solution.py:334
  169.4 1.0 copy.48
  170.4 2.1 %reshape.139 = f32[16,2,48,2,16]{4,3,2,0,1:T(2,128)S(1)} reshape(f32[16,2,1536]{2,0,1:T(8,128)S(1)} %copy.48) | data formatting | bytes 393216 | tf_op jit(solution)/shard_map/reshape | solution.py:348
  172.5 1.0 fusion.30
  173.5 0.1 pad_maximum_fusion
  173.6 0.6 copy.51
  174.2 1.2 reshape.140
  175.4 0.1 reshape.141
  175.6 2.8 %fusion.6 = f32[6,32,1280]{2,1,0:T(8,128)S(1)} fusion(bf16[6,256,1280]{2,1,0:T(8,128)(2,1)} %constant.102.clone.table_ref, bf16[32,6,256]{2,1,0:T(8,128)(2,1)S(1)} %reshape.141), kind=kOutput, calls=%fused_computation.13 | convolution fusion | flops 125829120 | bytes 5013504 | tf_op jit(solution)/shard_map/rgk,gkb->grb/dot_general | solution.py:360
  178.4 0.1 slice_add_fusion
  178.7 0.0 copy-start.2
  178.8 0.4 reshape.142
  179.1 1.1 copy.67
  180.2 0.0 all-to-all-done.3
  180.2 6.0 %all-to-all-start.2 = ((f32[16,16,480]{2,1,0:T(8,128)}), f32[16,16,480]{2,1,0:T(8,128)S(1)}, u32[]{:S(2)}, u32[]{:S(2)}) async-start(f32[16,16,480]{2,1,0:T(8,128)} %bitcast.149), calls=%async_computation.2 | async-start | bytes 1048576 | tf_op jit(solution)/shard_map/all_to_all | solution.py:416
  186.3 0.7 fusion.18
  186.9 1.2 custom-call.10
  188.1 0.2 fusion.21
  188.3 0.1 fusion.19
  188.5 0.1 reduce_sum.49
  188.6 0.0 copy-done.2
  188.6 0.8 fusion.31
  189.3 11.2 %all-to-all-done.2 = f32[16,16,480]{2,1,0:T(8,128)S(1)} async-done(((f32[16,16,480]{2,1,0:T(8,128)}), f32[16,16,480]{2,1,0:T(8,128)S(1)}, u32[]{:S(2)}, u32[]{:S(2)}) %all-to-all-start.2) | async-done | bytes 491552 | tf_op jit(solution)/shard_map/all_to_all | solution.py:416
  200.6 0.2 fusion.2
  200.8 0.6 fusion.24
  201.3 0.6 multiply_divide_fusion
  (40 shorter events, 0.5 us)
Async XLA Ops:
  13.1 7.6 %copy-start.3 = (s32[2,768]{1,0:T(2,128)S(1)}, s32[2,768]{1,0:T(2,128)}, u32[]{:S(2)}) copy-start(s32[2,768]{1,0:T(2,128)} %param.18) | copy-start | bytes 18436
  13.1 7.8 %copy-start.4 = (s32[768]{0:T(1024)S(1)}, s32[768]{0:T(1024)}, u32[]{:S(2)}) copy-start(s32[768]{0:T(1024)} %constant.116) | copy-start | bytes 9220
  13.1 46.2 %all-to-all-start = ((bf16[16,96,640]{2,1,0:T(8,128)(2,1)}), bf16[16,96,640]{2,1,0:T(8,128)(2,1)S(1)}, u32[]{:S(2)}, u32[]{:S(2)}) async-start(bf16[16,96,640]{2,1,0:T(8,128)(2,1)} %bitcast.152), calls=%async_computation | async-start | bytes 3932160 | tf_op jit(solution)/shard_map/all_to_all | solution.py:385
  59.3 1.3 copy-start.1
  66.6 61.8 %all-to-all-start.1 = ((bf16[16,96,640]{2,1,0:T(8,128)(2,1)}), bf16[16,96,640]{2,1,0:T(8,128)(2,1)S(1)}, u32[]{:S(2)}, u32[]{:S(2)}) async-start(bf16[16,96,640]{2,1,0:T(8,128)(2,1)} %fan_filter.1), calls=%async_computation.1 | async-start | bytes 3932160 | tf_op jit(solution)/shard_map/all_to_all | solution.py:401
  128.4 1.3 copy-start
  141.4 38.8 %all-to-all-start.3 = ((f32[16,1,680]{2,1,0:T(1,128)}), f32[16,1,680]{2,1,0:T(1,128)S(1)}, u32[]{:S(2)}, u32[]{:S(2)}) async-start(f32[16,1,680]{2,1,0:T(1,128)} %all_to_all.25), calls=%async_computation.3 | async-start | bytes 98304 | tf_op jit(solution)/shard_map/all_to_all | solution.py:409
  178.7 9.9 %copy-start.2 = (f32[680,480]{1,0:T(8,128)S(1)}, f32[680,480]{1,0:T(8,128)}, u32[]{:S(2)}) copy-start(f32[680,480]{1,0:T(8,128)} %constant.114.clone) | copy-start | bytes 3916804
  180.2 20.3 %all-to-all-start.2 = ((f32[16,16,480]{2,1,0:T(8,128)}), f32[16,16,480]{2,1,0:T(8,128)S(1)}, u32[]{:S(2)}, u32[]{:S(2)}) async-start(f32[16,16,480]{2,1,0:T(8,128)} %bitcast.149), calls=%async_computation.2 | async-start | bytes 1048576 | tf_op jit(solution)/shard_map/all_to_all | solution.py:416

commit v2 on v1

--- a/solution.py
+++ b/solution.py
@@ -80,109 +80,167 @@
     return np.broadcast_to(order, (order.shape[0], 2, fold)).reshape(-1)
 
 
-def spectrum_kernel(x_ref, table_ref, out_ref, y_ref):
+def spectrum_kernel(blocks, x_ref, table_ref, out_ref, y_ref):
     rows, readings = x_ref.shape
     width = readings // radix
-    for r0 in range(0, rows, 16):
-        rs = slice(r0, r0 + 16)
-        for b0 in range(0, width, lanes):
-            x = [
-                x_ref[rs, a * width + b0 : a * width + b0 + lanes].astype(f32)
-                for a in range(radix)
-            ]
-            yr = even_parts(x[0], x[half], [x[a] + x[radix - a] for a in range(1, half)])
-            ys = odd_parts([x[a] - x[radix - a] for a in range(1, half)])
-            left = slice(b0, b0 + lanes)
-            right = slice(width + b0, width + b0 + lanes)
-            y_ref[0, rs, left] = yr[0].astype(bf16)
-            y_ref[0, rs, right] = yr[half].astype(bf16)
-            for q in range(1, half):
-                y_ref[q, rs, left] = yr[q].astype(bf16)
-                y_ref[q, rs, right] = ys[q - 1].astype(bf16)
-    count = table_ref.shape[1]
-    for g in range(half):
-        out_ref[g * count : (g + 1) * count, :] = lax.dot_general(
-            table_ref[g], y_ref[g], (((1,), (1,)), ((), ())), preferred_element_type=f32
+    step = pl.program_id(0)
+
+    @pl.when(step < blocks)
+    def _():
+        @pl.loop(0, rows // 16)
+        def _(r):
+            rs = pl.ds(r * 16, 16)
+            ys = pl.ds(step * rows + r * 16, 16)
+            for b0 in range(0, width, lanes):
+                x = [
+                    x_ref[rs, a * width + b0 : a * width + b0 + lanes].astype(f32)
+                    for a in range(radix)
+                ]
+                even = even_parts(x[0], x[half], [x[a] + x[radix - a] for a in range(1, half)])
+                odd = odd_parts([x[a] - x[radix - a] for a in range(1, half)])
+                left = slice(b0, b0 + lanes)
+                right = slice(width + b0, width + b0 + lanes)
+                y_ref[0, ys, left] = even[0].astype(bf16)
+                y_ref[0, ys, right] = even[half].astype(bf16)
+                for q in range(1, half):
+                    y_ref[q, ys, left] = even[q].astype(bf16)
+                    y_ref[q, ys, right] = odd[q - 1].astype(bf16)
+
+    @pl.when(step >= blocks)
+    def _():
+        out_ref[...] = lax.dot_general(
+            table_ref[0],
+            y_ref[step - blocks],
+            (((1,), (1,)), ((), ())),
+            preferred_element_type=f32,
         ).astype(bf16)
 
 
 def time_spectrum(waveforms, table):
     channels, readings = waveforms.shape
     block = lanes if channels % lanes == 0 else channels
-    rows = table.shape[0] * table.shape[1]
+    blocks = channels // block
+    count = table.shape[1]
+    group = lambda i: jnp.maximum(i - blocks, 0)
     return pl.pallas_call(
-        spectrum_kernel,
-        out_shape=jax.ShapeDtypeStruct((rows, channels), bf16),
-        grid=(channels // block,),
+        functools.partial(spectrum_kernel, blocks),
+        out_shape=jax.ShapeDtypeStruct((half * count, channels), bf16),
+        grid=(blocks + half,),
         in_specs=[
-            pl.BlockSpec((block, readings), lambda i: (i, 0)),
-            pl.BlockSpec(table.shape, lambda i: (0, 0, 0)),
+            pl.BlockSpec((block, readings), lambda i: (jnp.minimum(i, blocks - 1), 0)),
+            pl.BlockSpec((1,) + table.shape[1:], lambda i: (group(i), 0, 0)),
         ],
-        out_specs=pl.BlockSpec((rows, block), lambda i: (0, i)),
-        scratch_shapes=[pltpu.VMEM((half, block, 2 * readings // radix), bf16)],
+        out_specs=pl.BlockSpec((count, channels), lambda i: (group(i), 0)),
+        scratch_shapes=[pltpu.VMEM((half, channels, 2 * readings // radix), bf16)],
         compiler_params=pltpu.CompilerParams(vmem_limit_bytes=vmem_limit),
         name="time_spectrum",
     )(waveforms, table)
 
 
-def power_kernel(f_ref, table_ref, out_ref, z_ref):
-    rows = f_ref.shape[1]
+def series_parts(zr, zs):
+    even = even_parts(zr[0], zs[0], zr[1:])
+    odd = odd_parts(zs[1:])
+    series = [even[0]]
+    series += [even[a] + odd[a - 1] for a in range(1, half)]
+    series += [even[half]]
+    series += [even[a] - odd[a - 1] for a in range(half - 1, 0, -1)]
+    return series
+
+
+def series_kernel(fold, b_ref, f_ref, t_ref, cos_ref, sin_ref, power_ref, out_ref, z_ref, c_ref):
+    group = pl.program_id(0)
+    taps, count = cos_ref.shape
+    rank = out_ref.shape[0]
     width = z_ref.shape[2] // 2
-    count = table_ref.shape[1]
-
-    @pl.when(pl.program_id(0) == 0)
+    z_ref[group] = lax.dot_general(
+        f_ref[...], t_ref[0], (((0,), (0,)), ((), ())), preferred_element_type=f32
+    )
+    sums = lax.dot_general(
+        b_ref[...], f_ref[...], (((1,), (1,)), ((), ())), preferred_element_type=f32
+    )
+    first, second = [], []
+    for r in range(rank):
+        member = sums[r * taps : (r + 1) * taps]
+        first.append(jnp.sum(member * cos_ref[...], axis=0, keepdims=True))
+        second.append(jnp.sum(member * sin_ref[...], axis=0, keepdims=True))
+    first = jnp.concatenate(first, axis=0)
+    second = jnp.concatenate(second, axis=0)
+    ids = lax.broadcasted_iota(jnp.int32, first.shape, 1)
+    spectra = first + jnp.where(
+        (ids // fold) % 2 == 0,
+        -pltpu.roll(second, count - fold, 1),
+        pltpu.roll(second, fold, 1),
+    )
+    high = spectra.astype(bf16)
+    low = (spectra - high.astype(f32)).astype(bf16)
+    c_ref[group] = jnp.dot(high, t_ref[0], preferred_element_type=f32) + jnp.dot(
+        low, t_ref[0], preferred_element_type=f32
+    )
+
+    @pl.when(group == half - 1)
     def _():
-        out_ref[...] = jnp.zeros_like(out_ref)
-
-    for g in range(half):
-        z_ref[g] = lax.dot_general(
-            f_ref[g * count : (g + 1) * count, :],
-            table_ref[g],
-            (((0,), (0,)), ((), ())),
-            preferred_element_type=f32,
+        power_ref[...] = jnp.zeros_like(power_ref)
+
+        @pl.loop(0, z_ref.shape[1] // 16)
+        def _(r):
+            rs = pl.ds(r * 16, 16)
+            for b0 in range(0, width, lanes):
+                left = slice(b0, b0 + lanes)
+                right = slice(width + b0, width + b0 + lanes)
+                parts = series_parts(
+                    [z_ref[g, rs, left] for g in range(half)],
+                    [z_ref[g, rs, right] for g in range(half)],
+                )
+                for a, value in enumerate(parts):
+                    square = value * value
+                    power_ref[a, :, left] += square[:8] + square[8:]
+
+        parts = series_parts(
+            [c_ref[g, :, :width] for g in range(half)],
+            [c_ref[g, :, width:] for g in range(half)],
         )
-    step = 16
-    for b0 in range(0, width, lanes):
-        left = slice(b0, b0 + lanes)
-        right = slice(width + b0, width + b0 + lanes)
-        for r0 in range(0, rows, step):
-            rs = slice(r0, r0 + step)
-            zr = [z_ref[g, rs, left] for g in range(half)]
-            zs = [z_ref[g, rs, right] for g in range(half)]
-            even = even_parts(zr[0], zs[0], zr[1:])
-            odd = odd_parts(zs[1:])
-            for a in range(radix):
-                m = min(a, radix - a)
-                value = even[m]
-                if 0 < a < half:
-                    value = value + odd[m - 1]
-                if a > half:
-                    value = value - odd[m - 1]
-                square = value * value
-                total = square[0:8]
-                for s in range(8, step, 8):
-                    total = total + square[s : s + 8]
-                out_ref[a, :, left] += total
-
-
-def time_power(filtered, table):
-    rows, channels = filtered.shape
-    block = lanes if channels % lanes == 0 else channels
-    width = table.shape[2] // 2
-    pieces = pl.pallas_call(
-        power_kernel,
-        out_shape=jax.ShapeDtypeStruct((radix, 8, width), f32),
-        grid=(channels // block,),
+        for a, value in enumerate(parts):
+            out_ref[:, a * width : (a + 1) * width] = value
+
+
+def power_and_series(turned, filtered, table, readings, fold):
+    rank, taps, channels = turned.shape
+    rows = filtered.shape[0]
+    count, width = table.shape[1], table.shape[2] // 2
+    bins = row_bins(rows // 2, fold)
+    angle = 2.0 * np.pi * (np.arange(taps)[:, None] * bins[None, :] % readings) / readings
+    power, series = pl.pallas_call(
+        functools.partial(series_kernel, fold),
+        out_shape=(
+            jax.ShapeDtypeStruct((radix, 8, width), f32),
+            jax.ShapeDtypeStruct((rank, readings), f32),
+        ),
+        grid=(half,),
         in_specs=[
-            pl.BlockSpec((rows, block), lambda i: (0, i)),
-            pl.BlockSpec(table.shape, lambda i: (0, 0, 0)),
+            pl.BlockSpec((rank * taps, channels), lambda i: (0, 0)),
+            pl.BlockSpec((count, channels), lambda i: (i, 0)),
+            pl.BlockSpec((1,) + table.shape[1:], lambda i: (i, 0, 0)),
+            pl.BlockSpec((taps, count), lambda i: (0, i)),
+            pl.BlockSpec((taps, count), lambda i: (0, i)),
         ],
-        out_specs=pl.BlockSpec((radix, 8, width), lambda i: (0, 0, 0)),
-        scratch_shapes=[pltpu.VMEM((half, block, 2 * width), f32)],
+        out_specs=(
+            pl.BlockSpec((radix, 8, width), lambda i: (0, 0, 0)),
+            pl.BlockSpec((rank, readings), lambda i: (0, 0)),
+        ),
+        scratch_shapes=[
+            pltpu.VMEM((half, channels, 2 * width), f32),
+            pltpu.VMEM((half, rank, 2 * width), f32),
+        ],
         compiler_params=pltpu.CompilerParams(vmem_limit_bytes=vmem_limit),
-        name="time_power",
-    )(filtered, table)
-    return jnp.sum(pieces, axis=1).reshape(-1)
+        name="power_and_series",
+    )(
+        turned.reshape(rank * taps, channels),
+        filtered,
+        table,
+        jnp.asarray(np.cos(angle), f32),
+        jnp.asarray(np.sin(angle), f32),
+    )
+    return jnp.sum(power, axis=1).reshape(-1), series
 
 
 def filter_tables(full_count, block_count, parts):
@@ -317,56 +375,29 @@
     return out.reshape(devices, rows, channels)
 
 
-def coefficient_kernel(b_ref, f_ref, cos_ref, sin_ref, out_ref):
-    sums = lax.dot_general(
-        b_ref[0], f_ref[...], (((1,), (1,)), ((), ())), preferred_element_type=f32
-    )
-    out_ref[0, 0:1, :] = jnp.sum(sums * cos_ref[...], axis=0, keepdims=True)
-    out_ref[0, 1:2, :] = jnp.sum(sums * sin_ref[...], axis=0, keepdims=True)
-
-
-def coefficient_spectra(turned, filtered, readings, fold):
-    rank, taps, channels = turned.shape
-    rows = filtered.shape[0]
-    bins = row_bins(rows // 2, fold)
-    angle = 2.0 * np.pi * (np.arange(taps)[:, None] * bins[None, :] % readings) / readings
-    whole = lambda i: (0, 0)
-    products = pl.pallas_call(
-        coefficient_kernel,
-        out_shape=jax.ShapeDtypeStruct((rank, 2, rows), f32),
-        grid=(rank,),
-        in_specs=[
-            pl.BlockSpec((1, taps, channels), lambda i: (i, 0, 0)),
-            pl.BlockSpec(filtered.shape, whole),
-            pl.BlockSpec(angle.shape, whole),
-            pl.BlockSpec(angle.shape, whole),
-        ],
-        out_specs=pl.BlockSpec((1, 2, rows), lambda i: (i, 0, 0)),
-        compiler_params=pltpu.CompilerParams(vmem_limit_bytes=vmem_limit),
-        name="coefficient_spectra",
-    )(turned, filtered, jnp.asarray(np.cos(angle), f32), jnp.asarray(np.sin(angle), f32))
-    parts = products.reshape(rank, 2, rows // (2 * fold), 2, fold)
-    real = parts[:, 0, :, 0] - parts[:, 1, :, 1]
-    imag = parts[:, 1, :, 0] + parts[:, 0, :, 1]
-    return jnp.stack([real, imag], axis=2).reshape(rank, rows)
-
-
-def lag_series(spectra, table):
-    rank = spectra.shape[0]
-    count, width = table.shape[1], table.shape[2] // 2
-    high = spectra.astype(bf16)
-    low = (spectra - high.astype(f32)).astype(bf16)
-    both = jnp.stack([high, low]).reshape(2 * rank, half, count)
-    z = jnp.einsum("rgk,gkb->grb", both, table, preferred_element_type=f32)
-    z = z[:, :rank] + z[:, rank:]
-    zr, zs = z[:, :, :width], z[:, :, width:]
-    even = even_parts(zr[0], zs[0], [zr[g] for g in range(1, half)])
-    odd = odd_parts([zs[g] for g in range(1, half)])
-    series = [even[0]]
-    series += [even[a] + odd[a - 1] for a in range(1, half)]
-    series += [even[half]]
-    series += [even[a] - odd[a - 1] for a in range(half - 1, 0, -1)]
-    return jnp.concatenate(series, axis=1)
+def final_kernel(full_count, taps, readings, got_ref, win_ref, gram_ref, det_ref, coef_ref):
+    lag_count = det_ref.shape[1]
+    rank = coef_ref.shape[0]
+    correlation = jnp.sum(got_ref[:, :rank, :], axis=0) * (2.0 / readings)
+    window = jnp.sum(win_ref[...], axis=0, keepdims=True)
+    row = lax.broadcasted_iota(jnp.int32, (window.shape[1], lag_count), 0)
+    lag = row - lax.broadcasted_iota(jnp.int32, row.shape, 1)
+    band = jnp.where((lag >= 0) & (lag < taps), 1.0, 0.0)
+    energy = jnp.dot(
+        jnp.broadcast_to(window, (8, window.shape[1])), band, precision=highest
+    )[:1] * (2.0 / readings) ** 2
+    level = energy / (full_count * taps) + 1e-06
+    gram = jnp.sum(gram_ref[...], axis=0)
+    solved = correlation
+    ids = lax.broadcasted_iota(jnp.int32, (rank, 1), 0)
+    for k in range(rank):
+        inverse = 1.0 / gram[k : k + 1, k : k + 1]
+        pivot_g, pivot_c = gram[k : k + 1] * inverse, solved[k : k + 1] * inverse
+        column = gram[:, k : k + 1]
+        gram = jnp.where(ids == k, pivot_g, gram - column * pivot_g)
+        solved = jnp.where(ids == k, pivot_c, solved - column * pivot_c)
+    det_ref[...] = jnp.sum(correlation * solved, axis=0, keepdims=True) / (rank * level)
+    coef_ref[...] = correlation / jnp.sqrt(level)
 
 
 def local(waveforms, basis, bounds):
@@ -385,45 +416,43 @@
     gathered = lax.all_to_all(spectrum, "chan", split_axis=0, concat_axis=0, tiled=True)
 
     flat = basis.reshape(rank, channels * taps)
-    gram_part = jnp.einsum("ka,ja->kj", flat, flat, preferred_element_type=f32)
-    gram = jnp.sum(lax.all_gather(gram_part, "chan"), axis=0)
-    factor = jnp.linalg.cholesky(gram)
-    inverse = jax.scipy.linalg.cho_solve((factor, True), jnp.eye(rank, dtype=f32))
+    gram = jnp.einsum("ka,ja->kj", flat, flat, preferred_element_type=f32)
     turned = jnp.swapaxes(basis, 1, 2)
 
     order = bin_order(frequencies)[0].reshape(-1)
     edges = lax.dynamic_slice_in_dim(bounds[:, order], position * bin_count, bin_count, 1)
     scale = jnp.asarray(np.where(order == 0, 0.5, 1.0) / full_count, f32).reshape(1, -1)
     scale = lax.dynamic_slice_in_dim(scale, position * bin_count, bin_count, 1)
+    scale, gram, turned = lax.optimization_barrier((scale, gram, turned))
     gathered = gathered.reshape(devices, 2 * bin_count, channels)
     apply = filter_fused if channels % lanes == 0 else filter_plain
     passed = apply(gathered, edges, scale, fold).reshape(2 * frequencies, channels)
     filtered = lax.all_to_all(passed, "chan", split_axis=0, concat_axis=0, tiled=True)
 
-    power = time_power(filtered, table)
-    extended = jnp.concatenate([power, power[:taps]])
-    windows = jnp.stack(
-        [extended[d * lag_count : (d + 1) * lag_count + taps] for d in range(devices)]
-    )
-    windows = jnp.sum(
-        lax.all_to_all(windows, "chan", split_axis=0, concat_axis=0, tiled=True),
-        axis=0,
-        keepdims=True,
-    )
-    spectra = coefficient_spectra(turned, filtered, readings, fold)
-    series = lag_series(spectra, table)
+    power, series = power_and_series(turned, filtered, table, readings, fold)
+    ahead = 1 + -(-taps // lag_count)
+    gram_rows = -(-rank * rank // lag_count)
+    power = power.reshape(devices, lag_count)
+    windows = jnp.stack([jnp.roll(power, -n, axis=0) for n in range(ahead)], axis=1)
+    gram = jnp.pad(gram.reshape(-1), (0, gram_rows * lag_count - rank * rank))
+    gram = jnp.broadcast_to(
+        gram.reshape(1, gram_rows, lag_count), (devices, gram_rows, lag_count)
+    )
     series = series.reshape(rank, devices, lag_count).transpose(1, 0, 2)
-    series = lax.all_to_all(series, "chan", split_axis=0, concat_axis=0, tiled=True)
-    correlation = jnp.sum(series, axis=0) * (2.0 / readings)
-
-    lag = np.arange(lag_count + taps)[:, None] - np.arange(lag_count)[None, :]
-    band = jnp.asarray((lag >= 0) & (lag < taps), f32)
-    energy = jnp.dot(windows, band, precision=highest)[0] * (2.0 / readings) ** 2
-    level = energy / (full_count * taps) + 1e-06
-    solved = jnp.dot(inverse, correlation, precision=highest)
-    detection = jnp.sum(correlation * solved, axis=0) / (rank * level)
-    coefficients = correlation / jnp.sqrt(level)[None, :]
-    return (detection, coefficients)
+    packed = jnp.concatenate([series, windows, gram], axis=1)
+    packed = lax.all_to_all(packed, "chan", split_axis=0, concat_axis=0, tiled=True)
+    windows = packed[:, rank : rank + ahead].reshape(devices, ahead * lag_count)
+    gram = packed[:, rank + ahead :].reshape(devices, -1)[:, : rank * rank]
+    detection, coefficients = pl.pallas_call(
+        functools.partial(final_kernel, full_count, taps, readings),
+        out_shape=(
+            jax.ShapeDtypeStruct((1, lag_count), f32),
+            jax.ShapeDtypeStruct((rank, lag_count), f32),
+        ),
+        compiler_params=pltpu.CompilerParams(vmem_limit_bytes=vmem_limit),
+        name="detect",
+    )(packed, windows, gram.reshape(devices, rank, rank))
+    return (detection[0], coefficients)
 
 
 def solution(mesh):

time: 203 us -> 182 us (0.90)
  waiting for transfers between devices: 46.1 us -> 68.4 us
  starting transfers between devices: 34.8 us -> 18.1 us
  blocking collectives: 43.7 us -> 30.6 us
  other arithmetic: 7.86 us -> 1.17 us
  matrix products: 9.2 us -> 5.09 us
  local copies, waits for them, and re-layouts: 13.6 us -> 10.1 us
    all_gather x1 -> x0, blocking collectives: 43.7 us -> none  [local(): gram = jnp.sum(lax.all_gather(gram_part, 'chan'), axis=0)]
    all_to_all x1, waiting for transfers between devices: 0.01 us -> 38.6 us  [local(): lax.all_to_all(passed, 'chan', split_axis=0, concat_axis=0, tiled=True)]
    all_to_all x0 -> x1, blocking collectives: none -> 30.6 us  [local(): lax.all_to_all(packed, 'chan', split_axis=0, concat_axis=0, tiled=True)]
    all_to_all x2 -> x0, starting transfers between devices: 16.6 us -> none  [the longest x1 10.6 us: local(): lax.all_to_all(windows, 'chan', split_axis=0, concat_axis=0, tiled=True)]
    all_to_all x2 -> x0, waiting for transfers between devices: 11.2 us -> none  [the longest x1 11.2 us: local(): lax.all_to_all(series, 'chan', split_axis=0, concat_axis=0, tiled=True)]
    all_to_all x1, waiting for transfers between devices: 35 us -> 29.8 us  [local(): lax.all_to_all(spectrum, 'chan', split_axis=0, concat_axis=0, tiled=True)]
    another operation x7 -> x0, other arithmetic: 4.08 us -> none  [the longest x3 2.13 us: local(): factor = jnp.linalg.cholesky(gram)]
    dot_general x4 -> x1, matrix products: 8.86 us -> 5.09 us  [local(): gram = jnp.einsum('ka,ja->kj', flat, flat, preferred_element_type=f32)]
  transfers between devices with their start and end apart: 4 -> 2, of which waited for: 2 -> 2; matrix products, arithmetic and copies ran while one was open for 12% -> 5% of each run, Pallas kernels for 9% -> 0%
where the time goes in v2:
time: 182 us; the launch traced here: 181 us
  waiting for transfers between devices  68.4 us (38%)
  Pallas kernels  46.8 us (26%)
  blocking collectives  30.6 us (17%)
  starting transfers between devices  18.1 us (10%)
  local copies, waits for them, and re-layouts  10.1 us (6%)
  matrix products  5.09 us (3%)
    all_to_all x1, waiting for transfers between devices, local(): lax.all_to_all(passed, 'chan', split_axis=0, concat_axis=0, tiled=True)  38.6 us
    all_to_all x1, blocking collectives, local(): lax.all_to_all(packed, 'chan', split_axis=0, concat_axis=0, tiled=True)  30.6 us
    all_to_all x1, waiting for transfers between devices, local(): lax.all_to_all(spectrum, 'chan', split_axis=0, concat_axis=0, tiled=True)  29.8 us
    pallas_call x1, Pallas kernels, power_and_series(): pl.pallas_call(functools.partial(series_kernel, fold), out_shape=(jax.Sha...  23.8 us
    pallas_call x1, Pallas kernels, time_spectrum(): pl.pallas_call(functools.partial(spectrum_kernel, blocks), out_shape=jax....  13.8 us
    all_to_all x1, starting transfers between devices, local(): lax.all_to_all(passed, 'chan', split_axis=0, concat_axis=0, tiled=True)  10.7 us
    all_to_all x1, starting transfers between devices, local(): lax.all_to_all(spectrum, 'chan', split_axis=0, concat_axis=0, tiled=True)  7.41 us
    pallas_call x1, Pallas kernels, filter_fused(): pl.pallas_call(functools.partial(filter_kernel, fold), out_shape=jax.Shap...  6 us
  transfers between devices with their start and end apart: 2, of which 2 were waited for; matrix products, arithmetic and copies ran while one was open for 5% of the time, Pallas kernels for 0%

profile of v2, /device:TPU:0, one launch (start us, length us, event | category | flops | bytes accessed | tf_op | source)
XLA Modules:
  0.0 181.1 jit_solution(16036128197645831540)
XLA Ops:
  0.6 13.8 %time_spectrum.1 = bf16[1536,640]{1,0:T(8,128)(2,1)} custom-call(bf16[640,7680]{1,0:T(8,128)(2,1)} %x_ref.1, bf16[6,256,1280]{2,1,0:T(8,128)(2,1)} %constant.38.clone.table_ref.t_ref), custom_call_target="tpu_custom_call" | custom-call | tf_op jit(solution)/shard_map/time_spectrum/pallas_call | solution.py:125
  14.5 7.4 %all-to-all-start = ((bf16[16,96,640]{2,1,0:T(8,128)(2,1)}), bf16[16,96,640]{2,1,0:T(8,128)(2,1)S(1)}, u32[]{:S(2)}, u32[]{:S(2)}) async-start(bf16[16,96,640]{2,1,0:T(8,128)(2,1)} %bitcast.16), calls=%async_computation | async-start | bytes 3932160 | tf_op jit(solution)/shard_map/all_to_all | solution.py:416
  21.9 0.0 copy-start.3
  21.9 0.0 copy-start.4
  21.9 1.3 dynamic-slice_bitcast_fusion.scale_ref
  23.2 5.1 %fusion.2 = f32[16,16]{1,0:T(8,128)S(1)} fusion(bf16[16,640,200]{1,2,0:T(8,128)(2,1)} %param.16), kind=kOutput, calls=%fused_computation.3 | convolution fusion | flops 65536000 | bytes 4097024 | tf_op jit(solution)/shard_map/ka,ja->kj/dot_general | solution.py:419
  28.3 0.0 copy-done.3
  28.3 0.2 copy.23
  28.5 0.0 copy-done.4
  28.5 1.6 gather_fusion
  30.1 0.6 copy.27
  30.8 29.8 %all-to-all-done.x_ref = bf16[16,96,640]{2,1,0:T(8,128)(2,1)S(1)} async-done(((bf16[16,96,640]{2,1,0:T(8,128)(2,1)}), bf16[16,96,640]{2,1,0:T(8,128)(2,1)S(1)}, u32[]{:S(2)}, u32[]{:S(2)}) %all-to-all-start) | async-done | bytes 1966112 | tf_op jit(solution)/shard_map/all_to_all | solution.py:416
  60.6 0.0 copy-start.1
  60.6 1.3 copy-done.1
  61.9 6.0 %fan_filter.1 = bf16[16,96,640]{2,1,0:T(8,128)(2,1)} custom-call(s32[2,48]{1,0:T(2,128)} %bitcast.21, f32[1,48]{1,0:T(1,128)} %dynamic-slice_bitcast_fusion.scale_ref, bf16[16,96,640]{2,1,0:T(8,128)(2,1)} %copy-done.1, bf16[160,160]{1,0:T(8,128)(2,1)} %constant.42.clone.w1_ref, bf16[256,256]{1,0:T(8,128)(2,1)} %constant.43.clone.w2_ref, ...), custom_call_target="tpu_custom_call" | custom-call | tf_op jit(solution)/shard_map/fan_filter/pallas_call | solution.py:334
  67.9 10.7 %all-to-all-start.1 = ((bf16[16,96,640]{2,1,0:T(8,128)(2,1)}), bf16[16,96,640]{2,1,0:T(8,128)(2,1)S(1)}, u32[]{:S(2)}, u32[]{:S(2)}) async-start(bf16[16,96,640]{2,1,0:T(8,128)(2,1)} %fan_filter.1), calls=%async_computation.1 | async-start | bytes 3932160 | tf_op jit(solution)/shard_map/all_to_all | solution.py:430
  78.6 0.1 reshape.40
  78.7 38.6 %all-to-all-done.1 = bf16[16,96,640]{2,1,0:T(8,128)(2,1)S(1)} async-done(((bf16[16,96,640]{2,1,0:T(8,128)(2,1)}), bf16[16,96,640]{2,1,0:T(8,128)(2,1)S(1)}, u32[]{:S(2)}, u32[]{:S(2)}) %all-to-all-start.1) | async-done | bytes 1966112 | tf_op jit(solution)/shard_map/all_to_all | solution.py:430
  117.3 0.0 copy-start
  117.3 1.3 copy-done
  118.6 23.8 %power_and_series.1 = (f32[12,8,640]{2,1,0:T(8,128)}, f32[16,7680]{1,0:T(8,128)}) custom-call(bf16[3200,640]{1,0:T(8,128)(2,1)} %bitcast.18, bf16[1536,640]{1,0:T(8,128)(2,1)} %bitcast.17, bf16[6,256,1280]{2,1,0:T(8,128)(2,1)} %constant.38.clone.table_ref.t_ref, f32[200,1536]{1,0:T(8,128)} %constant.48.clone.cos_ref, f32[200,1536]{1,0:T(8,128)} %constant.49.clone.sin_ref), custom_call_target="tpu_custom_call" | custom-call | tf_op jit(solution)/shard_map/power_and_series/pallas_call | solution.py:212
  142.4 1.0 reduce_sum.9
  143.4 0.1 reshape_reshape.3
  143.5 0.1 stack.6
  143.6 1.4 reshape.39
  145.1 0.3 copy.34
  145.4 0.1 pad_maximum_fusion
  145.6 30.6 %all_to_all.22.got_ref = f32[16,19,480]{2,1,0:T(8,128)S(1)} all-to-all(f32[16,19,480]{2,1,0:T(8,128)S(1)} %pad_maximum_fusion), channel_id=1, replica_groups=mesh['groups'=2,'chan'=16] {'chan'}, dimensions={0} | all-to-all | bytes 1167360 | tf_op jit(solution)/shard_map/all_to_all | solution.py:443
  176.2 0.0 copy-start.2
  176.2 0.9 reshape.43.gram_ref
  177.2 0.8 reshape.41.win_ref
  177.9 0.0 copy-done.2
  177.9 3.1 %detect.1 = (f32[1,480]{1,0:T(1,128)}, f32[16,480]{1,0:T(8,128)}) custom-call(f32[16,19,480]{2,1,0:T(8,128)} %copy-done.2, f32[16,960]{1,0:T(8,128)} %reshape.41.win_ref, f32[16,16,16]{2,1,0:T(8,128)} %reshape.43.gram_ref), custom_call_target="tpu_custom_call" | custom-call | tf_op jit(solution)/shard_map/detect/pallas_call | solution.py:446
  (12 shorter events, 0.1 us)
Async XLA Ops:
  14.5 46.1 %all-to-all-start = ((bf16[16,96,640]{2,1,0:T(8,128)(2,1)}), bf16[16,96,640]{2,1,0:T(8,128)(2,1)S(1)}, u32[]{:S(2)}, u32[]{:S(2)}) async-start(bf16[16,96,640]{2,1,0:T(8,128)(2,1)} %bitcast.16), calls=%async_computation | async-start | bytes 3932160 | tf_op jit(solution)/shard_map/all_to_all | solution.py:416
  21.9 6.4 %copy-start.3 = (s32[2,768]{1,0:T(2,128)S(1)}, s32[2,768]{1,0:T(2,128)}, u32[]{:S(2)}) copy-start(s32[2,768]{1,0:T(2,128)} %param.17) | copy-start | bytes 18436
  21.9 6.6 %copy-start.4 = (s32[768]{0:T(1024)S(1)}, s32[768]{0:T(1024)}, u32[]{:S(2)}) copy-start(s32[768]{0:T(1024)} %constant.53) | copy-start | bytes 9220
  60.6 1.3 copy-start.1
  67.9 49.4 %all-to-all-start.1 = ((bf16[16,96,640]{2,1,0:T(8,128)(2,1)}), bf16[16,96,640]{2,1,0:T(8,128)(2,1)S(1)}, u32[]{:S(2)}, u32[]{:S(2)}) async-start(bf16[16,96,640]{2,1,0:T(8,128)(2,1)} %fan_filter.1), calls=%async_computation.1 | async-start | bytes 3932160 | tf_op jit(solution)/shard_map/all_to_all | solution.py:430
  117.3 1.3 copy-start
  176.2 1.7 copy-start.2

commit v3 on v2

--- a/solution.py
+++ b/solution.py
@@ -375,11 +375,63 @@
     return out.reshape(devices, rows, channels)
 
 
-def final_kernel(full_count, taps, readings, got_ref, win_ref, gram_ref, det_ref, coef_ref):
-    lag_count = det_ref.shape[1]
-    rank = coef_ref.shape[0]
-    correlation = jnp.sum(got_ref[:, :rank, :], axis=0) * (2.0 / readings)
-    window = jnp.sum(win_ref[...], axis=0, keepdims=True)
+def greet(me, devices):
+    barrier = pltpu.get_barrier_semaphore()
+
+    @pl.loop(1, devices)
+    def _(off):
+        pl.semaphore_signal(barrier, inc=1, device_id={"chan": lax.rem(me + off, devices)})
+
+    pl.semaphore_wait(barrier, devices - 1)
+
+
+def final_kernel(
+    full_count, taps, readings, series_ref, extra_ref, det_ref, coef_ref, got_ref, more_ref, sent, came
+):
+    devices, rank, lag_count = series_ref.shape
+    square = rank * rank
+    span = extra_ref.shape[2] - square
+    me = lax.axis_index("chan")
+    greet(me, devices)
+
+    def copies(peer, slot):
+        pair = ((series_ref, got_ref), (extra_ref, more_ref))
+        return [
+            pltpu.make_async_remote_copy(
+                src_ref=src.at[peer],
+                dst_ref=dst.at[slot],
+                send_sem=sent.at[n, peer],
+                recv_sem=came.at[n, slot],
+                device_id={"chan": peer},
+            )
+            for n, (src, dst) in enumerate(pair)
+        ]
+
+    @pl.loop(1, devices)
+    def _(off):
+        for copy in copies(lax.rem(me + off, devices), me):
+            copy.start()
+
+    got_ref[me] = series_ref[me]
+    more_ref[me] = extra_ref[me]
+
+    @pl.loop(1, devices)
+    def _(off):
+        peer = lax.rem(me + off, devices)
+        for copy in copies(peer, peer):
+            copy.wait()
+
+    correlation = jnp.sum(got_ref[...].astype(f32), axis=0) * (2.0 / readings)
+    extra = jnp.sum(more_ref[...], axis=0)
+    window = extra[:, :span]
+    packed = jnp.broadcast_to(extra[:, span:], (rank, square))
+    spread = lax.broadcasted_iota(jnp.int32, packed.shape, 1)
+    packed = jnp.where(
+        spread // rank == lax.broadcasted_iota(jnp.int32, packed.shape, 0), packed, 0.0
+    )
+    pick = lax.broadcasted_iota(jnp.int32, (square, rank), 0) % rank
+    pick = jnp.where(pick == lax.broadcasted_iota(jnp.int32, pick.shape, 1), 1.0, 0.0)
+    gram = jnp.dot(packed, pick, precision=highest)
     row = lax.broadcasted_iota(jnp.int32, (window.shape[1], lag_count), 0)
     lag = row - lax.broadcasted_iota(jnp.int32, row.shape, 1)
     band = jnp.where((lag >= 0) & (lag < taps), 1.0, 0.0)
@@ -387,7 +439,6 @@
         jnp.broadcast_to(window, (8, window.shape[1])), band, precision=highest
     )[:1] * (2.0 / readings) ** 2
     level = energy / (full_count * taps) + 1e-06
-    gram = jnp.sum(gram_ref[...], axis=0)
     solved = correlation
     ids = lax.broadcasted_iota(jnp.int32, (rank, 1), 0)
     for k in range(rank):
@@ -431,27 +482,33 @@
 
     power, series = power_and_series(turned, filtered, table, readings, fold)
     ahead = 1 + -(-taps // lag_count)
-    gram_rows = -(-rank * rank // lag_count)
+    span = -(-(lag_count + taps) // lanes) * lanes
     power = power.reshape(devices, lag_count)
-    windows = jnp.stack([jnp.roll(power, -n, axis=0) for n in range(ahead)], axis=1)
-    gram = jnp.pad(gram.reshape(-1), (0, gram_rows * lag_count - rank * rank))
-    gram = jnp.broadcast_to(
-        gram.reshape(1, gram_rows, lag_count), (devices, gram_rows, lag_count)
-    )
-    series = series.reshape(rank, devices, lag_count).transpose(1, 0, 2)
-    packed = jnp.concatenate([series, windows, gram], axis=1)
-    packed = lax.all_to_all(packed, "chan", split_axis=0, concat_axis=0, tiled=True)
-    windows = packed[:, rank : rank + ahead].reshape(devices, ahead * lag_count)
-    gram = packed[:, rank + ahead :].reshape(devices, -1)[:, : rank * rank]
+    windows = jnp.concatenate([jnp.roll(power, -n, axis=0) for n in range(ahead)], axis=1)
+    windows = jnp.pad(windows[:, : lag_count + taps], ((0, 0), (0, span - lag_count - taps)))
+    gram = jnp.broadcast_to(gram.reshape(1, -1), (devices, rank * rank))
+    extra = jnp.concatenate([windows, gram], axis=1)[:, None, :]
+    series = series.astype(bf16).reshape(rank, devices, lag_count).transpose(1, 0, 2)
+    vmem = pl.BlockSpec(memory_space=pltpu.VMEM)
     detection, coefficients = pl.pallas_call(
         functools.partial(final_kernel, full_count, taps, readings),
         out_shape=(
             jax.ShapeDtypeStruct((1, lag_count), f32),
             jax.ShapeDtypeStruct((rank, lag_count), f32),
         ),
-        compiler_params=pltpu.CompilerParams(vmem_limit_bytes=vmem_limit),
+        in_specs=[vmem, vmem],
+        out_specs=(vmem, vmem),
+        scratch_shapes=[
+            pltpu.VMEM(series.shape, bf16),
+            pltpu.VMEM(extra.shape, f32),
+            pltpu.SemaphoreType.DMA((2, devices)),
+            pltpu.SemaphoreType.DMA((2, devices)),
+        ],
+        compiler_params=pltpu.CompilerParams(
+            vmem_limit_bytes=vmem_limit, collective_id=0, has_side_effects=True
+        ),
         name="detect",
-    )(packed, windows, gram.reshape(devices, rank, rank))
+    )(series, extra)
     return (detection[0], coefficients)
 
 

time: 182 us -> 169 us (0.929)
  blocking collectives: 30.6 us -> 0 us
  Pallas kernels: 46.8 us -> 62.8 us
    all_to_all x1 -> x0, blocking collectives: 30.6 us -> none  [local(): lax.all_to_all(packed, 'chan', split_axis=0, concat_axis=0, tiled=True)]
    pallas_call x1, Pallas kernels: 3.14 us -> 19.1 us  [local(): pl.pallas_call(functools.partial(final_kernel, full_count, taps, readings...]
    unnamed x14 -> x15, local copies, waits for them, and re-layouts: 3.49 us -> 6.1 us
    reshape x5 -> x2, local copies, waits for them, and re-layouts: 3.45 us -> 1.29 us  [local(): series.astype(bf16).reshape(rank, devices, lag_count).transpose(1, 0, 2)]
where the time goes in v3:
time: 169 us; the launch traced here: 168 us
  waiting for transfers between devices  68.4 us (40%)
  Pallas kernels  62.8 us (37%)
  starting transfers between devices  18.1 us (11%)
  local copies, waits for them, and re-layouts  11.1 us (7%)
  matrix products  5.09 us (3%)
  other arithmetic  2.16 us (1%)
    all_to_all x1, waiting for transfers between devices, local(): lax.all_to_all(passed, 'chan', split_axis=0, concat_axis=0, tiled=True)  38.6 us
    all_to_all x1, waiting for transfers between devices, local(): lax.all_to_all(spectrum, 'chan', split_axis=0, concat_axis=0, tiled=True)  29.8 us
    pallas_call x1, Pallas kernels, power_and_series(): pl.pallas_call(functools.partial(series_kernel, fold), out_shape=(jax.Sha...  23.8 us
    pallas_call x1, Pallas kernels, local(): pl.pallas_call(functools.partial(final_kernel, full_count, taps, readings...  19.1 us
    pallas_call x1, Pallas kernels, time_spectrum(): pl.pallas_call(functools.partial(spectrum_kernel, blocks), out_shape=jax....  13.8 us
    all_to_all x1, starting transfers between devices, local(): lax.all_to_all(passed, 'chan', split_axis=0, concat_axis=0, tiled=True)  10.7 us
    all_to_all x1, starting transfers between devices, local(): lax.all_to_all(spectrum, 'chan', split_axis=0, concat_axis=0, tiled=True)  7.41 us
    unnamed x15, local copies, waits for them, and re-layouts  6.1 us
  transfers between devices with their start and end apart: 2, of which 2 were waited for; matrix products, arithmetic and copies ran while one was open for 5% of the time, Pallas kernels for 0%

profile of v3, /device:TPU:0, one launch (start us, length us, event | category | flops | bytes accessed | tf_op | source)
XLA Modules:
  0.0 168.4 jit_solution(1258974030184173412)
XLA Ops:
  0.6 13.8 %time_spectrum.1 = bf16[1536,640]{1,0:T(8,128)(2,1)} custom-call(bf16[640,7680]{1,0:T(8,128)(2,1)} %x_ref.1, bf16[6,256,1280]{2,1,0:T(8,128)(2,1)} %constant.40.clone.table_ref.t_ref), custom_call_target="tpu_custom_call" | custom-call | tf_op jit(solution)/shard_map/time_spectrum/pallas_call | solution.py:125
  14.5 7.4 %all-to-all-start = ((bf16[16,96,640]{2,1,0:T(8,128)(2,1)}), bf16[16,96,640]{2,1,0:T(8,128)(2,1)S(1)}, u32[]{:S(2)}, u32[]{:S(2)}) async-start(bf16[16,96,640]{2,1,0:T(8,128)(2,1)} %bitcast.13), calls=%async_computation | async-start | bytes 3932160 | tf_op jit(solution)/shard_map/all_to_all | solution.py:467
  21.9 0.0 copy-start.2
  21.9 0.0 copy-start.3
  21.9 1.3 dynamic-slice_bitcast_fusion.scale_ref
  23.2 5.1 %fusion.2 = f32[16,16]{1,0:T(8,128)S(1)} fusion(bf16[16,640,200]{1,2,0:T(8,128)(2,1)} %param.16), kind=kOutput, calls=%fused_computation.3 | convolution fusion | flops 65536000 | bytes 4097024 | tf_op jit(solution)/shard_map/ka,ja->kj/dot_general | solution.py:470
  28.3 0.0 copy-done.2
  28.3 0.2 copy.23
  28.5 0.0 copy-done.3
  28.5 1.6 gather_fusion
  30.1 0.6 copy.26
  30.8 29.8 %all-to-all-done.x_ref = bf16[16,96,640]{2,1,0:T(8,128)(2,1)S(1)} async-done(((bf16[16,96,640]{2,1,0:T(8,128)(2,1)}), bf16[16,96,640]{2,1,0:T(8,128)(2,1)S(1)}, u32[]{:S(2)}, u32[]{:S(2)}) %all-to-all-start) | async-done | bytes 1966112 | tf_op jit(solution)/shard_map/all_to_all | solution.py:467
  60.6 0.0 copy-start.1
  60.6 1.3 copy-done.1
  61.9 6.0 %fan_filter.1 = bf16[16,96,640]{2,1,0:T(8,128)(2,1)} custom-call(s32[2,48]{1,0:T(2,128)} %bitcast.17, f32[1,48]{1,0:T(1,128)} %dynamic-slice_bitcast_fusion.scale_ref, bf16[16,96,640]{2,1,0:T(8,128)(2,1)} %copy-done.1, bf16[160,160]{1,0:T(8,128)(2,1)} %constant.44.clone.w1_ref, bf16[256,256]{1,0:T(8,128)(2,1)} %constant.45.clone.w2_ref, ...), custom_call_target="tpu_custom_call" | custom-call | tf_op jit(solution)/shard_map/fan_filter/pallas_call | solution.py:334
  67.9 10.7 %all-to-all-start.1 = ((bf16[16,96,640]{2,1,0:T(8,128)(2,1)}), bf16[16,96,640]{2,1,0:T(8,128)(2,1)S(1)}, u32[]{:S(2)}, u32[]{:S(2)}) async-start(bf16[16,96,640]{2,1,0:T(8,128)(2,1)} %fan_filter.1), calls=%async_computation.1 | async-start | bytes 3932160 | tf_op jit(solution)/shard_map/all_to_all | solution.py:481
  78.6 0.1 reshape.34
  78.7 38.6 %all-to-all-done.1 = bf16[16,96,640]{2,1,0:T(8,128)(2,1)S(1)} async-done(((bf16[16,96,640]{2,1,0:T(8,128)(2,1)}), bf16[16,96,640]{2,1,0:T(8,128)(2,1)S(1)}, u32[]{:S(2)}, u32[]{:S(2)}) %all-to-all-start.1) | async-done | bytes 1966112 | tf_op jit(solution)/shard_map/all_to_all | solution.py:481
  117.3 0.0 copy-start
  117.3 1.3 copy-done
  118.6 0.0 copy-start.4
  118.6 23.8 %power_and_series.1 = (f32[12,8,640]{2,1,0:T(8,128)}, f32[16,7680]{1,0:T(8,128)}) custom-call(bf16[3200,640]{1,0:T(8,128)(2,1)} %bitcast.15, bf16[1536,640]{1,0:T(8,128)(2,1)} %bitcast.14, bf16[6,256,1280]{2,1,0:T(8,128)(2,1)} %constant.40.clone.table_ref.t_ref, f32[200,1536]{1,0:T(8,128)} %constant.50.clone.cos_ref, f32[200,1536]{1,0:T(8,128)} %constant.51.clone.sin_ref), custom_call_target="tpu_custom_call" | custom-call | tf_op jit(solution)/shard_map/power_and_series/pallas_call | solution.py:212
  142.4 1.0 reduce_sum.9
  143.4 0.1 reshape_reshape.3
  143.5 1.1 convert_element_type.5
  144.6 0.4 reshape.24
  145.0 0.8 copy.32
  145.9 0.0 copy-done.4
  145.9 0.1 fusion.5
  146.0 0.7 broadcast_in_dim.16.extra_ref
  146.6 19.1 %detect.1 = (f32[1,480]{1,0:T(1,128)}, f32[16,480]{1,0:T(8,128)}) custom-call(bf16[16,16,480]{2,1,0:T(8,128)(2,1)} %bitcast.16, f32[16,1,1024]{2,1,0:T(1,128)} %broadcast_in_dim.16.extra_ref), custom_call_target="tpu_custom_call" | custom-call | tf_op jit(solution)/shard_map/detect/pallas_call | solution.py:493
  165.8 1.2 copy.35
  167.0 1.4 copy.36
  (6 shorter events, 0.0 us)
Async XLA Ops:
  14.5 46.1 %all-to-all-start = ((bf16[16,96,640]{2,1,0:T(8,128)(2,1)}), bf16[16,96,640]{2,1,0:T(8,128)(2,1)S(1)}, u32[]{:S(2)}, u32[]{:S(2)}) async-start(bf16[16,96,640]{2,1,0:T(8,128)(2,1)} %bitcast.13), calls=%async_computation | async-start | bytes 3932160 | tf_op jit(solution)/shard_map/all_to_all | solution.py:467
  21.9 6.4 %copy-start.2 = (s32[2,768]{1,0:T(2,128)S(1)}, s32[2,768]{1,0:T(2,128)}, u32[]{:S(2)}) copy-start(s32[2,768]{1,0:T(2,128)} %param.17) | copy-start | bytes 18436
  21.9 6.6 %copy-start.3 = (s32[768]{0:T(1024)S(1)}, s32[768]{0:T(1024)}, u32[]{:S(2)}) copy-start(s32[768]{0:T(1024)} %constant.53) | copy-start | bytes 9220
  60.6 1.3 copy-start.1
  67.9 49.4 %all-to-all-start.1 = ((bf16[16,96,640]{2,1,0:T(8,128)(2,1)}), bf16[16,96,640]{2,1,0:T(8,128)(2,1)S(1)}, u32[]{:S(2)}, u32[]{:S(2)}) async-start(bf16[16,96,640]{2,1,0:T(8,128)(2,1)} %fan_filter.1), calls=%async_computation.1 | async-start | bytes 3932160 | tf_op jit(solution)/shard_map/all_to_all | solution.py:481
  117.3 1.3 copy-start
  118.6 27.3 %copy-start.4 = (pred[768]{0:T(1024)(128)(4,1)S(1)}, pred[768]{0:T(1024)(128)(4,1)}, u32[]{:S(2)}) copy-start(pred[768]{0:T(1024)(128)(4,1)} %constant.38.clone.1) | copy-start | bytes 2308

commit v4 on v3

--- a/solution.py
+++ b/solution.py
@@ -267,8 +267,7 @@
     )
 
 
-def filter_kernel(fold, edges_ref, scale_ref, x_ref, w1_ref, w2_ref, v1_ref, v2_ref, tw_ref, mag_ref, o_ref):
-    step = pl.program_id(0)
+def filter_chunk(fold, step, edges_ref, scale_ref, x_ref, w1_ref, w2_ref, v1_ref, v2_ref, tw_ref, mag_ref, o_ref):
     devices = x_ref.shape[0]
     parts = x_ref.shape[2] // lanes
     n1 = mag_ref.shape[0]
@@ -325,21 +324,84 @@
             ).astype(bf16)
 
 
-def filter_fused(gathered, edges, scale, fold):
-    devices, rows, channels = gathered.shape
+def greet(me, devices):
+    barrier = pltpu.get_barrier_semaphore()
+
+    @pl.loop(1, devices)
+    def _(off):
+        pl.semaphore_signal(barrier, inc=1, device_id={"chan": lax.rem(me + off, devices)})
+
+    pl.semaphore_wait(barrier, devices - 1)
+
+
+def filter_kernel(fold, edges_ref, scale_ref, x_ref, *refs):
+    tables, (out_ref, got_ref, mid_ref, sent, came) = refs[:6], refs[6:]
+    devices, rows, _ = x_ref.shape
+    chunks = rows // (2 * fold)
+    me = lax.axis_index("chan")
+    greet(me, devices)
+
+    def piece(k):
+        return pl.ds(pl.multiple_of(k * (2 * fold), 2 * fold), 2 * fold)
+
+    def copy(way, k, peer, slot):
+        src, dst = ((x_ref, got_ref), (mid_ref, out_ref))[way]
+        return pltpu.make_async_remote_copy(
+            src_ref=src.at[peer, piece(k)],
+            dst_ref=dst.at[slot, piece(k)],
+            send_sem=sent.at[way, k, peer],
+            recv_sem=came.at[way, k, slot],
+            device_id={"chan": peer},
+        )
+
+    def others(body):
+        @pl.loop(1, devices)
+        def _(off):
+            body(lax.rem(me + off, devices))
+
+    @pl.loop(0, chunks)
+    def _(k):
+        others(lambda peer: copy(0, k, peer, me).start())
+
+    got_ref[me] = x_ref[me]
+
+    @pl.loop(0, chunks)
+    def _(k):
+        others(lambda peer: copy(0, k, peer, peer).wait_recv())
+        filter_chunk(
+            fold, k, edges_ref, scale_ref, got_ref.at[:, piece(k), :], *tables, mid_ref.at[:, piece(k), :]
+        )
+        others(lambda peer: copy(1, k, peer, me).start())
+        out_ref[me, piece(k), :] = mid_ref[me, piece(k), :]
+
+    @pl.loop(0, chunks)
+    def _(k):
+        others(lambda peer: copy(0, k, peer, peer).wait_send())
+        others(lambda peer: copy(1, k, peer, peer).wait())
+
+
+def filter_exchange(spectrum, edges, scale, fold):
+    devices, rows, channels = spectrum.shape
     tables = filter_tables(devices * channels, devices, channels // lanes)
-    whole = [pl.BlockSpec(t.shape, lambda i, n=t.ndim: (0,) * n) for t in tables]
-    block = pl.BlockSpec((devices, 2 * fold, channels), lambda i: (0, i, 0))
     smem = pl.BlockSpec(memory_space=pltpu.SMEM)
+    vmem = pl.BlockSpec(memory_space=pltpu.VMEM)
+    sems = (2, rows // (2 * fold), devices)
     return pl.pallas_call(
         functools.partial(filter_kernel, fold),
-        out_shape=jax.ShapeDtypeStruct(gathered.shape, bf16),
-        grid=(rows // (2 * fold),),
-        in_specs=[smem, smem, block] + whole,
-        out_specs=block,
-        compiler_params=pltpu.CompilerParams(vmem_limit_bytes=vmem_limit),
+        out_shape=jax.ShapeDtypeStruct(spectrum.shape, bf16),
+        in_specs=[smem, smem] + [vmem] * (1 + len(tables)),
+        out_specs=vmem,
+        scratch_shapes=[
+            pltpu.VMEM(spectrum.shape, bf16),
+            pltpu.VMEM(spectrum.shape, bf16),
+            pltpu.SemaphoreType.DMA(sems),
+            pltpu.SemaphoreType.DMA(sems),
+        ],
+        compiler_params=pltpu.CompilerParams(
+            vmem_limit_bytes=vmem_limit, collective_id=1, has_side_effects=True
+        ),
         name="fan_filter",
-    )(edges, scale, gathered, *tables)
+    )(edges, scale, spectrum, *tables)
 
 
 def filter_plain(gathered, edges, scale, fold):
@@ -373,16 +435,6 @@
     out = (jnp.stack(pair) * scale[0][None, :, None, None]).astype(bf16)
     out = out.reshape(2, rows // (2 * fold), fold, devices, channels).transpose(3, 1, 0, 2, 4)
     return out.reshape(devices, rows, channels)
-
-
-def greet(me, devices):
-    barrier = pltpu.get_barrier_semaphore()
-
-    @pl.loop(1, devices)
-    def _(off):
-        pl.semaphore_signal(barrier, inc=1, device_id={"chan": lax.rem(me + off, devices)})
-
-    pl.semaphore_wait(barrier, devices - 1)
 
 
 def final_kernel(
@@ -464,8 +516,6 @@
 
     table = jnp.asarray(time_table(frequencies, readings, fold), bf16)
     spectrum = time_spectrum(waveforms, table)
-    gathered = lax.all_to_all(spectrum, "chan", split_axis=0, concat_axis=0, tiled=True)
-
     flat = basis.reshape(rank, channels * taps)
     gram = jnp.einsum("ka,ja->kj", flat, flat, preferred_element_type=f32)
     turned = jnp.swapaxes(basis, 1, 2)
@@ -474,11 +524,14 @@
     edges = lax.dynamic_slice_in_dim(bounds[:, order], position * bin_count, bin_count, 1)
     scale = jnp.asarray(np.where(order == 0, 0.5, 1.0) / full_count, f32).reshape(1, -1)
     scale = lax.dynamic_slice_in_dim(scale, position * bin_count, bin_count, 1)
-    scale, gram, turned = lax.optimization_barrier((scale, gram, turned))
-    gathered = gathered.reshape(devices, 2 * bin_count, channels)
-    apply = filter_fused if channels % lanes == 0 else filter_plain
-    passed = apply(gathered, edges, scale, fold).reshape(2 * frequencies, channels)
-    filtered = lax.all_to_all(passed, "chan", split_axis=0, concat_axis=0, tiled=True)
+    spectrum = spectrum.reshape(devices, 2 * bin_count, channels)
+    if channels % lanes == 0:
+        filtered = filter_exchange(spectrum, edges, scale, fold)
+    else:
+        gathered = lax.all_to_all(spectrum, "chan", split_axis=0, concat_axis=0, tiled=True)
+        passed = filter_plain(gathered, edges, scale, fold)
+        filtered = lax.all_to_all(passed, "chan", split_axis=0, concat_axis=0, tiled=True)
+    filtered = filtered.reshape(2 * frequencies, channels)
 
     power, series = power_and_series(turned, filtered, table, readings, fold)
     ahead = 1 + -(-taps // lag_count)

time: 169 us -> 165 us (0.976)
  Pallas kernels: 62.8 us -> 147 us
  waiting for transfers between devices: 68.4 us -> 0 us
  starting transfers between devices: 18.1 us -> 0 us
  local copies, waits for them, and re-layouts: 11.1 us -> 9.14 us
    pallas_call x1, Pallas kernels: 6 us -> 91 us  [filter_exchange(): pl.pallas_call(functools.partial(filter_kernel, fold), out_shape=jax.Shap...]
    all_to_all x2 -> x0, waiting for transfers between devices: 68.4 us -> none  [the longest x1 38.6 us: local(): lax.all_to_all(passed, 'chan', split_axis=0, concat_axis=0, tiled=True)]
    all_to_all x2 -> x0, starting transfers between devices: 18.1 us -> none  [the longest x1 10.7 us: local(): lax.all_to_all(passed, 'chan', split_axis=0, concat_axis=0, tiled=True)]
    unnamed x15 -> x9, local copies, waits for them, and re-layouts: 6.1 us -> 4.15 us
  transfers between devices with their start and end apart: 2 -> 0, of which waited for: 2 -> 0; matrix products, arithmetic and copies ran while one was open for 5% -> 0% of each run, Pallas kernels for 0% -> 0%
where the time goes in v4:
time: 165 us; the launch traced here: 164 us
  Pallas kernels  147 us (89%)
  local copies, waits for them, and re-layouts  9.14 us (6%)
  matrix products  5.09 us (3%)
  other arithmetic  1.88 us (1%)
    pallas_call x1, Pallas kernels, filter_exchange(): pl.pallas_call(functools.partial(filter_kernel, fold), out_shape=jax.Shap...  91 us
    pallas_call x1, Pallas kernels, power_and_series(): pl.pallas_call(functools.partial(series_kernel, fold), out_shape=(jax.Sha...  23.8 us
    pallas_call x1, Pallas kernels, local(): pl.pallas_call(functools.partial(final_kernel, full_count, taps, readings...  18.2 us
    pallas_call x1, Pallas kernels, time_spectrum(): pl.pallas_call(functools.partial(spectrum_kernel, blocks), out_shape=jax....  13.8 us
    dot_general x1, matrix products, local(): gram = jnp.einsum('ka,ja->kj', flat, flat, preferred_element_type=f32)  5.09 us
    unnamed x9, local copies, waits for them, and re-layouts  4.15 us

profile of v4, /device:TPU:0, one launch (start us, length us, event | category | flops | bytes accessed | tf_op | source)
XLA Modules:
  0.0 163.6 jit_solution(6889613227001446169)
XLA Ops:
  0.6 0.9 copy.21
  1.5 0.7 pad_clamp_fusion
  2.2 1.6 gather_fusion
  3.8 0.6 copy.26
  4.4 1.3 dynamic-slice_bitcast_fusion.scale_ref
  5.7 13.8 %time_spectrum.1 = bf16[1536,640]{1,0:T(8,128)(2,1)} custom-call(bf16[640,7680]{1,0:T(8,128)(2,1)} %x_ref.1, bf16[6,256,1280]{2,1,0:T(8,128)(2,1)} %constant.40.clone.table_ref.t_ref), custom_call_target="tpu_custom_call" | custom-call | tf_op jit(solution)/shard_map/time_spectrum/pallas_call | solution.py:125
  19.5 91.0 %fan_filter.1 = bf16[16,96,640]{2,1,0:T(8,128)(2,1)} custom-call(s32[2,48]{1,0:T(2,128)} %bitcast.18, f32[1,48]{1,0:T(1,128)} %dynamic-slice_bitcast_fusion.scale_ref, bf16[16,96,640]{2,1,0:T(8,128)(2,1)} %bitcast.15, bf16[160,160]{1,0:T(8,128)(2,1)} %constant.44.clone.refs_0_, bf16[256,256]{1,0:T(8,128)(2,1)} %constant.45.clone.refs_1_, ...), custom_call_target="tpu_custom_call" | custom-call | tf_op jit(solution)/shard_map/fan_filter/pallas_call | solution.py:389
  110.5 0.0 copy-start.1
  110.5 23.8 %power_and_series.1 = (f32[12,8,640]{2,1,0:T(8,128)}, f32[16,7680]{1,0:T(8,128)}) custom-call(bf16[3200,640]{1,0:T(8,128)(2,1)} %bitcast.16, bf16[1536,640]{1,0:T(8,128)(2,1)} %bitcast.14, bf16[6,256,1280]{2,1,0:T(8,128)(2,1)} %constant.40.clone.table_ref.t_ref, f32[200,1536]{1,0:T(8,128)} %constant.50.clone.cos_ref, f32[200,1536]{1,0:T(8,128)} %constant.51.clone.sin_ref), custom_call_target="tpu_custom_call" | custom-call | tf_op jit(solution)/shard_map/power_and_series/pallas_call | solution.py:212
  134.3 0.0 copy-start
  134.3 1.1 reduce_sum.9
  135.3 0.1 reshape_reshape.3
  135.4 0.0 copy-done.1
  135.5 0.1 fusion.5
  135.5 5.1 %fusion.2 = f32[16,16]{1,0:T(8,128)S(1)} fusion(bf16[16,640,200]{1,2,0:T(8,128)(2,1)} %param.16), kind=kOutput, calls=%fused_computation.3 | convolution fusion | flops 65536000 | bytes 4097024 | tf_op jit(solution)/shard_map/ka,ja->kj/dot_general | solution.py:520
  140.6 0.1 reshape.34
  140.8 0.7 broadcast_in_dim.16.extra_ref
  141.4 0.0 copy-done
  141.5 0.4 reshape.24
  141.9 0.8 copy.32
  142.8 18.2 %detect.1 = (f32[1,480]{1,0:T(1,128)}, f32[16,480]{1,0:T(8,128)}) custom-call(bf16[16,16,480]{2,1,0:T(8,128)(2,1)} %bitcast.17, f32[16,1,1024]{2,1,0:T(1,128)} %broadcast_in_dim.16.extra_ref), custom_call_target="tpu_custom_call" | custom-call | tf_op jit(solution)/shard_map/detect/pallas_call | solution.py:546
  161.0 1.2 copy.35
  162.2 1.4 copy.36
  (6 shorter events, 0.1 us)
Async XLA Ops:
  110.5 25.0 %copy-start.1 = (pred[768]{0:T(1024)(128)(4,1)S(1)}, pred[768]{0:T(1024)(128)(4,1)}, u32[]{:S(2)}) copy-start(pred[768]{0:T(1024)(128)(4,1)} %constant.38.clone.1) | copy-start | bytes 2308
  134.3 7.2 %copy-start = (f32[16,7680]{1,0:T(8,128)S(1)}, f32[16,7680]{1,0:T(8,128)}, u32[]{:S(2)}) copy-start(f32[16,7680]{1,0:T(8,128)} %get-tuple-element.6) | copy-start | bytes 1474564

commit v5 on v4

--- a/solution.py
+++ b/solution.py
@@ -147,22 +147,20 @@
     return series
 
 
-def series_kernel(fold, b_ref, f_ref, t_ref, cos_ref, sin_ref, power_ref, out_ref, z_ref, c_ref):
-    group = pl.program_id(0)
-    taps, count = cos_ref.shape
-    rank = out_ref.shape[0]
-    width = z_ref.shape[2] // 2
+def series_group(fold, group, block, b_ref, table, cos, sin, z_ref, c_ref):
+    taps, count = cos.shape
+    rank = c_ref.shape[1]
     z_ref[group] = lax.dot_general(
-        f_ref[...], t_ref[0], (((0,), (0,)), ((), ())), preferred_element_type=f32
+        block, table, (((0,), (0,)), ((), ())), preferred_element_type=f32
     )
     sums = lax.dot_general(
-        b_ref[...], f_ref[...], (((1,), (1,)), ((), ())), preferred_element_type=f32
+        b_ref[...], block, (((1,), (1,)), ((), ())), preferred_element_type=f32
     )
     first, second = [], []
     for r in range(rank):
         member = sums[r * taps : (r + 1) * taps]
-        first.append(jnp.sum(member * cos_ref[...], axis=0, keepdims=True))
-        second.append(jnp.sum(member * sin_ref[...], axis=0, keepdims=True))
+        first.append(jnp.sum(member * cos, axis=0, keepdims=True))
+        second.append(jnp.sum(member * sin, axis=0, keepdims=True))
     first = jnp.concatenate(first, axis=0)
     second = jnp.concatenate(second, axis=0)
     ids = lax.broadcasted_iota(jnp.int32, first.shape, 1)
@@ -173,34 +171,46 @@
     )
     high = spectra.astype(bf16)
     low = (spectra - high.astype(f32)).astype(bf16)
-    c_ref[group] = jnp.dot(high, t_ref[0], preferred_element_type=f32) + jnp.dot(
-        low, t_ref[0], preferred_element_type=f32
+    c_ref[group] = jnp.dot(high, table, preferred_element_type=f32) + jnp.dot(
+        low, table, preferred_element_type=f32
+    )
+
+
+def series_end(power_ref, out_ref, z_ref, c_ref):
+    width = z_ref.shape[2] // 2
+    power_ref[...] = jnp.zeros_like(power_ref)
+
+    @pl.loop(0, z_ref.shape[1] // 16)
+    def _(r):
+        rs = pl.ds(r * 16, 16)
+        for b0 in range(0, width, lanes):
+            left = slice(b0, b0 + lanes)
+            right = slice(width + b0, width + b0 + lanes)
+            parts = series_parts(
+                [z_ref[g, rs, left] for g in range(half)],
+                [z_ref[g, rs, right] for g in range(half)],
+            )
+            for a, value in enumerate(parts):
+                square = value * value
+                power_ref[a, :, left] += square[:8] + square[8:]
+
+    parts = series_parts(
+        [c_ref[g, :, :width] for g in range(half)],
+        [c_ref[g, :, width:] for g in range(half)],
+    )
+    for a, value in enumerate(parts):
+        out_ref[:, a * width : (a + 1) * width] = value
+
+
+def series_kernel(fold, b_ref, f_ref, t_ref, cos_ref, sin_ref, power_ref, out_ref, z_ref, c_ref):
+    group = pl.program_id(0)
+    series_group(
+        fold, group, f_ref[...], b_ref, t_ref[0], cos_ref[...], sin_ref[...], z_ref, c_ref
     )
 
     @pl.when(group == half - 1)
     def _():
-        power_ref[...] = jnp.zeros_like(power_ref)
-
-        @pl.loop(0, z_ref.shape[1] // 16)
-        def _(r):
-            rs = pl.ds(r * 16, 16)
-            for b0 in range(0, width, lanes):
-                left = slice(b0, b0 + lanes)
-                right = slice(width + b0, width + b0 + lanes)
-                parts = series_parts(
-                    [z_ref[g, rs, left] for g in range(half)],
-                    [z_ref[g, rs, right] for g in range(half)],
-                )
-                for a, value in enumerate(parts):
-                    square = value * value
-                    power_ref[a, :, left] += square[:8] + square[8:]
-
-        parts = series_parts(
-            [c_ref[g, :, :width] for g in range(half)],
-            [c_ref[g, :, width:] for g in range(half)],
-        )
-        for a, value in enumerate(parts):
-            out_ref[:, a * width : (a + 1) * width] = value
+        series_end(power_ref, out_ref, z_ref, c_ref)
 
 
 def power_and_series(turned, filtered, table, readings, fold):
@@ -335,20 +345,20 @@
 
 
 def filter_kernel(fold, edges_ref, scale_ref, x_ref, *refs):
-    tables, (out_ref, got_ref, mid_ref, sent, came) = refs[:6], refs[6:]
-    devices, rows, _ = x_ref.shape
-    chunks = rows // (2 * fold)
+    tables, refs = refs[:6], refs[6:]
+    b_ref, t_ref, cos_ref, sin_ref, power_ref, series_ref, *refs = refs
+    got_ref, mid_ref, out_ref, z_ref, c_ref, sent, came = refs
+    chunks, devices, rows, channels = x_ref.shape
+    per_chunk = half // chunks
+    count = t_ref.shape[1]
     me = lax.axis_index("chan")
     greet(me, devices)
-
-    def piece(k):
-        return pl.ds(pl.multiple_of(k * (2 * fold), 2 * fold), 2 * fold)
 
     def copy(way, k, peer, slot):
         src, dst = ((x_ref, got_ref), (mid_ref, out_ref))[way]
         return pltpu.make_async_remote_copy(
-            src_ref=src.at[peer, piece(k)],
-            dst_ref=dst.at[slot, piece(k)],
+            src_ref=src.at[k, peer],
+            dst_ref=dst.at[k, slot],
             send_sem=sent.at[way, k, peer],
             recv_sem=came.at[way, k, slot],
             device_id={"chan": peer},
@@ -362,38 +372,61 @@
     @pl.loop(0, chunks)
     def _(k):
         others(lambda peer: copy(0, k, peer, me).start())
-
-    got_ref[me] = x_ref[me]
+        got_ref[k, me] = x_ref[k, me]
 
     @pl.loop(0, chunks)
     def _(k):
         others(lambda peer: copy(0, k, peer, peer).wait_recv())
         filter_chunk(
-            fold, k, edges_ref, scale_ref, got_ref.at[:, piece(k), :], *tables, mid_ref.at[:, piece(k), :]
+            fold, k, edges_ref, scale_ref, got_ref.at[k], *tables, mid_ref.at[k]
         )
         others(lambda peer: copy(1, k, peer, me).start())
-        out_ref[me, piece(k), :] = mid_ref[me, piece(k), :]
+        out_ref[k, me] = mid_ref[k, me]
+
+    @pl.loop(0, chunks)
+    def _(k):
+        others(lambda peer: copy(1, k, peer, peer).wait_recv())
+        for n in range(per_chunk):
+            part = devices // per_chunk
+            block = out_ref[k, n * part : (n + 1) * part].reshape(count, channels)
+            group = k * per_chunk + n
+            series_group(
+                fold, group, block, b_ref, t_ref[group], cos_ref[group], sin_ref[group], z_ref, c_ref
+            )
+
+    series_end(power_ref, series_ref, z_ref, c_ref)
 
     @pl.loop(0, chunks)
     def _(k):
         others(lambda peer: copy(0, k, peer, peer).wait_send())
-        others(lambda peer: copy(1, k, peer, peer).wait())
-
-
-def filter_exchange(spectrum, edges, scale, fold):
-    devices, rows, channels = spectrum.shape
+        others(lambda peer: copy(1, k, peer, peer).wait_send())
+
+
+def filter_exchange(spectrum, edges, scale, turned, table, readings, fold):
+    chunks, devices, rows, channels = spectrum.shape
+    rank, taps, _ = turned.shape
+    count, width = table.shape[1], table.shape[2] // 2
+    bins = row_bins(chunks * devices * fold, fold)
+    angle = 2.0 * np.pi * (np.arange(taps)[:, None] * bins[None, :] % readings) / readings
+    angle = angle.reshape(taps, half, count).transpose(1, 0, 2)
     tables = filter_tables(devices * channels, devices, channels // lanes)
     smem = pl.BlockSpec(memory_space=pltpu.SMEM)
     vmem = pl.BlockSpec(memory_space=pltpu.VMEM)
-    sems = (2, rows // (2 * fold), devices)
-    return pl.pallas_call(
+    sems = (2, chunks, devices)
+    power, series = pl.pallas_call(
         functools.partial(filter_kernel, fold),
-        out_shape=jax.ShapeDtypeStruct(spectrum.shape, bf16),
-        in_specs=[smem, smem] + [vmem] * (1 + len(tables)),
-        out_specs=vmem,
+        out_shape=(
+            jax.ShapeDtypeStruct((radix, 8, width), f32),
+            jax.ShapeDtypeStruct((rank, readings), f32),
+        ),
+        in_specs=[smem, smem] + [vmem] * (5 + len(tables)),
+        out_specs=(vmem, vmem),
         scratch_shapes=[
             pltpu.VMEM(spectrum.shape, bf16),
             pltpu.VMEM(spectrum.shape, bf16),
+            pltpu.VMEM(spectrum.shape, bf16),
+            pltpu.VMEM((half, channels, 2 * width), f32),
+            pltpu.VMEM((half, rank, 2 * width), f32),
             pltpu.SemaphoreType.DMA(sems),
             pltpu.SemaphoreType.DMA(sems),
         ],
@@ -401,7 +434,17 @@
             vmem_limit_bytes=vmem_limit, collective_id=1, has_side_effects=True
         ),
         name="fan_filter",
-    )(edges, scale, spectrum, *tables)
+    )(
+        edges,
+        scale,
+        spectrum,
+        *tables,
+        turned.reshape(rank * taps, channels),
+        table,
+        jnp.asarray(np.cos(angle), f32),
+        jnp.asarray(np.sin(angle), f32),
+    )
+    return jnp.sum(power, axis=1).reshape(-1), series
 
 
 def filter_plain(gathered, edges, scale, fold):
@@ -521,19 +564,23 @@
     turned = jnp.swapaxes(basis, 1, 2)
 
     order = bin_order(frequencies)[0].reshape(-1)
+    chunks = bin_count // fold
+    fused = channels % lanes == 0 and half % chunks == 0 and devices % (half // chunks) == 0
+    if fused:
+        order = order.reshape(chunks, devices, fold).transpose(1, 0, 2).reshape(-1)
     edges = lax.dynamic_slice_in_dim(bounds[:, order], position * bin_count, bin_count, 1)
     scale = jnp.asarray(np.where(order == 0, 0.5, 1.0) / full_count, f32).reshape(1, -1)
     scale = lax.dynamic_slice_in_dim(scale, position * bin_count, bin_count, 1)
-    spectrum = spectrum.reshape(devices, 2 * bin_count, channels)
-    if channels % lanes == 0:
-        filtered = filter_exchange(spectrum, edges, scale, fold)
+    if fused:
+        spectrum = spectrum.reshape(chunks, devices, 2 * fold, channels)
+        power, series = filter_exchange(spectrum, edges, scale, turned, table, readings, fold)
     else:
+        spectrum = spectrum.reshape(devices, 2 * bin_count, channels)
         gathered = lax.all_to_all(spectrum, "chan", split_axis=0, concat_axis=0, tiled=True)
         passed = filter_plain(gathered, edges, scale, fold)
         filtered = lax.all_to_all(passed, "chan", split_axis=0, concat_axis=0, tiled=True)
-    filtered = filtered.reshape(2 * frequencies, channels)
-
-    power, series = power_and_series(turned, filtered, table, readings, fold)
+        filtered = filtered.reshape(2 * frequencies, channels)
+        power, series = power_and_series(turned, filtered, table, readings, fold)
     ahead = 1 + -(-taps // lag_count)
     span = -(-(lag_count + taps) // lanes) * lanes
     power = power.reshape(devices, lag_count)

time: 165 us -> 156 us (0.945)
  Pallas kernels: 147 us -> 139 us
    pallas_call x2 -> x1, Pallas kernels: 115 us -> 106 us  [filter_exchange(): pl.pallas_call(functools.partial(filter_kernel, fold), out_shape=(jax.Sha...]
where the time goes in v5:
time: 156 us; the launch traced here: 155 us
  Pallas kernels  139 us (89%)
  local copies, waits for them, and re-layouts  9.14 us (6%)
  matrix products  5.1 us (3%)
  other arithmetic  1.88 us (1%)
    pallas_call x1, Pallas kernels, filter_exchange(): pl.pallas_call(functools.partial(filter_kernel, fold), out_shape=(jax.Sha...  106 us
    pallas_call x1, Pallas kernels, local(): pl.pallas_call(functools.partial(final_kernel, full_count, taps, readings...  18.8 us
    pallas_call x1, Pallas kernels, time_spectrum(): pl.pallas_call(functools.partial(spectrum_kernel, blocks), out_shape=jax....  13.8 us
    dot_general x1, matrix products, local(): gram = jnp.einsum('ka,ja->kj', flat, flat, preferred_element_type=f32)  5.1 us
    unnamed x9, local copies, waits for them, and re-layouts  4.14 us

profile of v5, /device:TPU:0, one launch (start us, length us, event | category | flops | bytes accessed | tf_op | source)
XLA Modules:
  0.0 155.4 jit_solution(8454855824682361870)
XLA Ops:
  0.6 0.9 copy.21
  1.5 0.7 pad_clamp_fusion
  2.2 1.6 %gather_fusion = s32[768,2]{1,0:T(8,128)S(1)} fusion(s32[2,768]{0,1:T(8,128)S(1)} %copy.21, s32[1024]{0:T(1024)S(1)} %pad_clamp_fusion), kind=kCustom, calls=%fused_computation | custom fusion | bytes 15360 | tf_op jit(solution)/shard_map/gather | solution.py:571
  3.8 0.6 copy.26
  4.4 1.3 dynamic-slice_bitcast_fusion.scale_ref
  5.7 13.8 %time_spectrum.1 = bf16[1536,640]{1,0:T(8,128)(2,1)} custom-call(bf16[640,7680]{1,0:T(8,128)(2,1)} %x_ref.1, bf16[6,256,1280]{2,1,0:T(8,128)(2,1)} %constant.40.clone.table_ref.refs_7_), custom_call_target="tpu_custom_call" | custom-call | tf_op jit(solution)/shard_map/time_spectrum/pallas_call | solution.py:125
  19.5 0.0 copy-start.1
  19.5 106.0 %fan_filter.1 = (f32[12,8,640]{2,1,0:T(8,128)}, f32[16,7680]{1,0:T(8,128)}) custom-call(s32[2,48]{1,0:T(2,128)} %bitcast.16, f32[1,48]{1,0:T(1,128)} %dynamic-slice_bitcast_fusion.scale_ref, bf16[3,16,32,640]{3,2,1,0:T(8,128)(2,1)} %bitcast.13, bf16[160,160]{1,0:T(8,128)(2,1)} %constant.44.clone.refs_0_, bf16[256,256]{1,0:T(8,128)(2,1)} %constant.45.clone.refs_1_, ...), custom_call_target="tpu_custom_call" | custom-call | tf_op jit(solution)/shard_map/fan_filter/pallas_call | solution.py:416
  125.5 0.0 copy-start
  125.5 1.1 reduce_sum.9
  126.6 0.1 reshape_reshape.3
  126.7 0.0 copy-done.1
  126.7 0.1 fusion.5
  126.8 5.1 %fusion.2 = f32[16,16]{1,0:T(8,128)S(1)} fusion(bf16[16,640,200]{1,2,0:T(8,128)(2,1)} %param.16), kind=kOutput, calls=%fused_computation.3 | convolution fusion | flops 65536000 | bytes 4097024 | tf_op jit(solution)/shard_map/ka,ja->kj/dot_general | solution.py:563
  131.9 0.1 reshape.30
  132.0 0.7 broadcast_in_dim.16.extra_ref
  132.7 0.0 copy-done
  132.7 0.4 reshape.20
  133.2 0.8 copy.32
  134.0 18.8 %detect.1 = (f32[1,480]{1,0:T(1,128)}, f32[16,480]{1,0:T(8,128)}) custom-call(bf16[16,16,480]{2,1,0:T(8,128)(2,1)} %bitcast.15, f32[16,1,1024]{2,1,0:T(1,128)} %broadcast_in_dim.16.extra_ref), custom_call_target="tpu_custom_call" | custom-call | tf_op jit(solution)/shard_map/detect/pallas_call | solution.py:593
  152.8 1.2 copy.35
  154.1 1.4 copy.36
  (6 shorter events, 0.1 us)
Async XLA Ops:
  19.5 107.2 %copy-start.1 = (pred[768]{0:T(1024)(128)(4,1)S(1)}, pred[768]{0:T(1024)(128)(4,1)}, u32[]{:S(2)}) copy-start(pred[768]{0:T(1024)(128)(4,1)} %constant.38.clone.1) | copy-start | bytes 2308
  125.5 7.2 %copy-start = (f32[16,7680]{1,0:T(8,128)S(1)}, f32[16,7680]{1,0:T(8,128)}, u32[]{:S(2)}) copy-start(f32[16,7680]{1,0:T(8,128)} %get-tuple-element.6) | copy-start | bytes 1474564
